TPU v7x, 32 devices: a whole 2x2x4 slice. The times are simulated.
32 devices in a mesh: vocab: 8 (over z, x), dp: 4 (over y, core).
Axes of the slice: x: 2, y: 2, z: 4, core: 2. Of those that a mesh axis runs over, the one named last changes fastest.
Arguments:
- teacher_hidden: bfloat16 [512, 5376], P('dp'), may hold values from -48 to 48
- student_hidden: bfloat16 [512, 2560], P('dp'), may hold values from -48 to 48
- teacher_codes: bfloat16 [16384, 5376], P(('vocab', 'dp')), may hold values from -8 to 7, as said below
- teacher_scales: float32 [16384, 42], P(('vocab', 'dp')), may hold values from 0.003 to 0.07
- student_weight: bfloat16 [16384, 2560], P(('vocab', 'dp')), may hold values from -1 to 1
- loss_scale: bfloat16 [512], P('dp'), may hold values from 2 to 20
Outputs:
- kl: float32 [512], P('dp')
- grad_hidden: bfloat16 [512, 2560], P('dp', 'vocab')
- grad_weight: bfloat16 [16384, 2560], P(('vocab', 'dp'))
Inputs may be any that keep to these rules, and one draw needn't show every extreme that they name: `teacher_codes`: whole numbers.
All inputs are finite; a program needn't handle non-finite values.
Results may differ from a plain program's by a relative error of at most 0.0085.
Values may be sent and summed in bfloat16 or wider, within the bound.
A program may use at most 128 MiB of HBM per device.

v0:
```python
import functools

import jax
import jax.numpy as jnp
from jax import lax
from jax.experimental import pallas as pl
from jax.experimental.pallas import tpu as pltpu
from jax.sharding import PartitionSpec as P

GROUP = 128
LANE = 128
MESH = pl.DeviceIdType.MESH


def step_width(cols):
    units = cols // 256
    per = max(k for k in (1, 2, 3, 5, 7) if units % k == 0)
    return per * 256


def dot_t(left_rows, right_rows):
    return lax.dot_general(
        left_rows, right_rows, (((1,), (1,)), ((), ())), preferred_element_type=jnp.float32
    )


def kernel(
    n_vocab, n_dp,
    th_own, sh_own, codes, scales, weight, loss_in,
    kl_out, gh_out, gw_out,
    th, sh, table, wgt, wgt_t, tlog, slog, lsc, stat, stat_b, fin, in_a, in_b,
    grad, gw_buf, mine, theirs, core_in,
    y1s, y1r, x1s, x1r, x2s, x2r, y2s, y2r, zs, zr, zf,
    sc_rows, loss_row, ld_sem, gw_sem, pc_s, pc_r, hop_s, hop_r,
    ls_s, ls_r, a_s, a_r, b_s, b_r, cs, cr, r1s, r1r, r2s, r2r, z_ss, z_rs,
):
    v, d = lax.axis_index("vocab"), lax.axis_index("dp")
    c, y = lax.rem(d, 2), lax.div(d, 2)
    p, q = lax.rem(v, 2), lax.div(v, 2)
    n_y, n_z = n_dp // 2, n_vocab // 2
    n_off = n_y - 1
    mate = 2 * y + 1 - c
    v_pair = 2 * q + 1 - p
    r = lax.rem(q, 2)
    v_quad = 2 * (q + 1 - 2 * r) + p
    tok = th_own.shape[0]
    rv = zr.shape[1]
    n_z1 = n_z // 2

    def rcopy(src, dst, send, recv, dev):
        return pltpu.make_async_remote_copy(
            src_ref=src, dst_ref=dst, send_sem=send, recv_sem=recv,
            device_id=dev, device_id_type=MESH,
        )

    chunks = []
    for own, scr, tab, acc in ((th_own, th, table, tlog), (sh_own, sh, wgt, slog)):
        width = step_width(own.shape[1])
        for base in range(0, own.shape[1], width):
            chunks.append((own, scr, tab, acc, base, width))
    n_ch = len(chunks)

    loads = []
    for k, (own, scr, tab, acc, base, width) in enumerate(chunks):
        src = codes if tab is table else weight
        cp = pltpu.make_async_copy(
            src.at[:, pl.ds(base, width)], tab.at[:, pl.ds(base, width)], ld_sem.at[k]
        )
        cp.start()
        loads.append(cp)
    own_rows = pl.ds(pl.multiple_of(d * tok, tok), tok)
    own_loads = [
        pltpu.make_async_copy(th_own, th.at[own_rows], ld_sem.at[n_ch]),
        pltpu.make_async_copy(sh_own, sh.at[own_rows], ld_sem.at[n_ch + 1]),
    ]
    for cp in own_loads:
        cp.start()

    peers_a = []
    for dv in range(2):
        for dd in range(n_dp):
            if dv or dd:
                peers_a.append((v if dv == 0 else v_pair, lax.rem(d + dd, n_dp)))
    from_a = []
    peers_b = [(2 * lax.rem(q + o, n_z) + p, d) for o in range(1, n_z)]
    barrier = pltpu.get_barrier_semaphore()
    for peer in peers_a + peers_b:
        pl.semaphore_signal(barrier, inc=1, device_id=peer, device_id_type=MESH)
    pl.semaphore_wait(barrier, len(peers_a) + len(peers_b))

    quarter = tok // 4

    def rows(block):
        return pl.ds(pl.multiple_of(block * tok, tok), tok)

    def region(k, block, piece, half=None):
        scr, base, width = chunks[k][1], chunks[k][4], chunks[k][5]
        first, size = block * tok + piece * quarter, quarter
        if half is not None:
            size = quarter // 2
            first += half * size
        return scr.at[pl.ds(pl.multiple_of(first, size), size), pl.ds(base, width)]

    A, B, C, E = 2 * r + p, 2 * r + 1 - p, 2 * (1 - r) + p, 2 * (1 - r) + 1 - p
    X, Z = (v_pair, d), (v_quad, d)
    Y_A, Y_E, X_A, Z_A, X_C, Z_B, D_A, D_B, D_C, D_E = range(10)

    def far_by_y(k):
        return k > 0 and k % 2 == 0

    def came(o):
        return lax.rem(y + n_y - o, n_y)

    def y_send(k, o, kind):
        own, base, width = chunks[k][0], chunks[k][4], chunks[k][5]
        piece = A if kind == Y_A else E
        src = own.at[pl.ds(pl.multiple_of(piece * quarter, quarter), quarter), pl.ds(base, width)]
        to = 2 * lax.rem(y + o, n_y) + c
        return rcopy(
            src, region(k, d, piece), hop_s.at[kind, o - 1, k], hop_r.at[kind, o - 1, k], (v, to)
        )

    def hop(kind, k, o, side, piece, dev, half=None):
        ref = region(k, 2 * came(o) + side, piece, half)
        return rcopy(ref, ref, hop_s.at[kind, o - 1, k], hop_r.at[kind, o - 1, k], dev)

    def to_mate(kind, k, o, piece):
        launch(hop(kind, k, o, c, piece, (v, mate)))

    def launch(cp):
        cp.start()
        sends.append(cp)

    def stage_y(k):
        for o in range(1, n_y):
            hop(Y_A, k, o, c, A, X).wait_recv()
            launch(hop(X_A, k, o, c, A, X))
            launch(hop(Z_A, k, o, c, A, Z))
            to_mate(D_A, k, o, A)

    def stage_xz(k):
        for o in range(1, n_y):
            hop(X_A, k, o, c, B, X).wait_recv()
            if not far_by_y(k):
                launch(hop(Z_B, k, o, c, B, Z, 1))
            to_mate(D_B, k, o, B)
            hop(Z_A, k, o, c, C, Z).wait_recv()
            if not far_by_y(k):
                launch(hop(X_C, k, o, c, C, X, 0))
            to_mate(D_C, k, o, C)

    def stage_far(k):
        for o in range(1, n_y):
            if far_by_y(k):
                hop(Y_E, k, o, c, E, X).wait_recv()
            else:
                hop(X_C, k, o, c, E, X, 0).wait_recv()
                hop(Z_B, k, o, c, E, Z, 1).wait_recv()
            to_mate(D_E, k, o, E)

    def stage_mate(k):
        for o in range(1, n_y):
            for kind, piece in ((D_A, A), (D_B, B), (D_C, C), (D_E, E)):
                hop(kind, k, o, 1 - c, piece, X).wait_recv()

    sends = []
    mate_copies = [
        rcopy(th_own, th.at[own_rows], pc_s.at[0], pc_r.at[0], (v, mate)),
        rcopy(sh_own, sh.at[own_rows], pc_s.at[1], pc_r.at[1], (v, mate)),
    ]
    for k in range(n_ch):
        for o in range(1, n_y):
            launch(y_send(k, o, Y_A))
            if far_by_y(k):
                launch(y_send(k, o, Y_E))
        if k == 0:
            for cp in mate_copies:
                cp.start()
    loss_copies = []
    loss_row[...] = jnp.broadcast_to(
        loss_in[...].astype(jnp.float32).reshape(1, tok), loss_row.shape
    )
    lsc[d] = loss_row[...]
    groups = scales.shape[0]
    pad = jnp.zeros((sc_rows.shape[1] - groups, LANE), jnp.float32)
    for b in range(0, scales.shape[1], LANE):
        sc_rows[pl.ds(b, LANE), :] = jnp.concatenate(
            [scales[:, pl.ds(b, LANE)], pad], axis=0
        ).T

    def product(k, chip, first):
        own, scr, tab, acc, base, width = chunks[k]
        two = pl.ds(pl.multiple_of(chip * 2 * tok, 2 * tok), 2 * tok)
        part = dot_t(tab[:, pl.ds(base, width)], scr[two, pl.ds(base, width)])
        if first:
            acc[:, two] = part
        else:
            acc[:, two] += part

    def prepare(k):
        own, scr, tab, acc, base, width = chunks[k]
        loads[k].wait()
        if tab is table:
            @pl.loop(0, table.shape[0] // 64)
            def _(i):
                rsl = pl.ds(pl.multiple_of(i * 64, 64), 64)
                sc = sc_rows[rsl, :]
                for g in range(width // GROUP):
                    lane = pl.ds(base + g * GROUP, GROUP)
                    col = (base + g * GROUP) // GROUP
                    wide = table[rsl, lane].astype(jnp.float32) * sc[:, col : col + 1]
                    table[rsl, lane] = wide.astype(jnp.bfloat16)

    for cp in own_loads:
        cp.wait()
    firsts = [k == 0 or chunks[k][3] is not chunks[k - 1][3] for k in range(n_ch)]
    lag = 3
    for k in range(n_ch + lag):
        if k < n_ch:
            prepare(k)
            stage_y(k)
        if 1 <= k <= n_ch:
            stage_xz(k - 1)
        if 2 <= k <= n_ch + 1:
            stage_far(k - 2)
        if k < n_ch:
            if k == 0:
                for which, (own, scr) in enumerate(((th_own, th), (sh_own, sh))):
                    land = scr.at[rows(mate)]
                    rcopy(own, land, pc_s.at[which], pc_r.at[which], (v, mate)).wait_recv()
            product(k, y, firsts[k])
        if k >= lag:
            stage_mate(k - lag)
            if n_y > 1:
                @pl.loop(1, n_y)
                def _(o):
                    product(k - lag, lax.rem(y + n_y - o, n_y), firsts[k - lag])
        if k == n_ch - 1:
            for dd in range(1, n_dp):
                cp = rcopy(
                    loss_row, lsc.at[d], ls_s.at[dd - 1], ls_r.at[dd - 1],
                    (v, lax.rem(d + dd, n_dp)),
                )
                cp.start()
                loss_copies.append(cp)

    n_tok = n_dp * tok

    @pl.loop(0, n_dp)
    def _(j):
        sl = pl.ds(pl.multiple_of(j * tok, tok), tok)
        t_max = jnp.max(tlog[:, sl], axis=0, keepdims=True)
        s_max = jnp.max(slog[:, sl], axis=0, keepdims=True)
        te = jnp.exp(tlog[:, sl] - t_max)
        t_sum = jnp.sum(te, axis=0, keepdims=True)
        x_sum = jnp.sum(te * (tlog[:, sl] - slog[:, sl]), axis=0, keepdims=True)
        tlog[:, sl] = te
        se = jnp.exp(slog[:, sl] - s_max)
        s_sum = jnp.sum(se, axis=0, keepdims=True)
        slog[:, sl] = se
        stat[:, sl] = jnp.concatenate(
            [t_max, t_sum, x_sum, s_max, s_sum, jnp.zeros((3, tok), jnp.float32)], axis=0
        )

    def merge(parts):
        t_top = functools.reduce(jnp.maximum, [x[0:1] for x in parts])
        s_top = functools.reduce(jnp.maximum, [x[3:4] for x in parts])
        t_sum = x_sum = s_sum = 0.0
        for x in parts:
            t_w = jnp.exp(x[0:1] - t_top)
            t_sum += x[1:2] * t_w
            x_sum += x[2:3] * t_w
            s_sum += x[4:5] * jnp.exp(x[3:4] - s_top)
        return t_top, t_sum, x_sum, s_top, s_sum

    for i, peer in enumerate(peers_a):
        cp = rcopy(stat, in_a.at[i], a_s.at[i], a_r.at[i], peer)
        cp.start()
        sends.append(cp)
    for b in range(0, wgt.shape[1], 256):
        wgt_t[pl.ds(b, 256), :] = wgt[:, pl.ds(b, 256)].T
    for i, peer in enumerate(peers_a):
        rcopy(stat, in_a.at[i], a_s.at[i], a_r.at[i], peer).wait_recv()
    stat_b[...] = jnp.concatenate(
        list(merge([stat[...]] + [in_a[i] for i in range(len(peers_a))]))
        + [jnp.zeros((3, n_tok), jnp.float32)], axis=0
    )
    for i, peer in enumerate(peers_b):
        cp = rcopy(stat_b, in_b.at[i], b_s.at[i], b_r.at[i], peer)
        cp.start()
        sends.append(cp)
    for dd in range(1, n_dp):
        other = lax.rem(d + n_dp - dd, n_dp)
        rcopy(loss_row, lsc.at[other], ls_s.at[dd - 1], ls_r.at[dd - 1], (v, mate)).wait_recv()
    for i, peer in enumerate(peers_b):
        rcopy(stat_b, in_b.at[i], b_s.at[i], b_r.at[i], peer).wait_recv()
    t_top, t_sum, x_sum, s_top, s_sum = merge(
        [stat_b[...]] + [in_b[i] for i in range(len(peers_b))]
    )
    t_lse = t_top + jnp.log(t_sum)
    s_lse = s_top + jnp.log(s_sum)
    fin[...] = jnp.concatenate(
        [
            x_sum / t_sum - t_lse + s_lse,
            jnp.exp(stat[0:1] - t_lse),
            jnp.exp(stat[3:4] - s_lse),
            jnp.zeros((5, n_tok), jnp.float32),
        ],
        axis=0,
    )
    kl_out[...] = fin[0:1, own_rows]

    @pl.loop(0, n_dp)
    def _(j):
        sl = pl.ds(pl.multiple_of(j * tok, tok), tok)
        f = fin[:, sl]
        grad[:, sl] = (
            lsc[j][0:1] * (slog[:, sl] * f[2:3] - tlog[:, sl] * f[1:2])
        ).astype(jnp.bfloat16)

    order = []
    for i in range(n_z1):
        order += [i, n_z1 + i]
    order += [i for i in range(n_z) if i not in order]

    def hidden_part(z):
        for pp in range(2):
            feat = wgt_t[pl.ds((2 * z + pp) * rv, rv), :]
            for yy in range(n_y):
                part = jnp.dot(
                    feat, grad[:, pl.ds(yy * 2 * tok, 2 * tok)],
                    preferred_element_type=jnp.float32,
                )
                left, right = part[:, :tok], part[:, tok:]
                mine[z, pp, yy] = jnp.where(c == 0, left, right)
                theirs[z, pp, yy] = jnp.where(c == 0, right, left).astype(jnp.bfloat16)

    def core_copy(z):
        return rcopy(theirs.at[z], core_in.at[z], cs.at[z], cr.at[z], (v, mate))

    def y1_copy(z, o):
        to = 2 * lax.rem(y + o, n_y) + c
        return rcopy(
            y1s.at[z, o - 1], y1r.at[z, o - 1], r1s.at[z, o - 1], r1r.at[z, o - 1], (v, to)
        )

    def x1_copy(z):
        return rcopy(x1s.at[z], x1r.at[z], r2s.at[z, 0], r2r.at[z, 0], (v_pair, d))

    def x2_copy(z):
        return rcopy(
            x2s.at[z - n_z1], x2r.at[z - n_z1], r1s.at[z, 0], r1r.at[z, 0], (v_pair, d)
        )

    def y2_copy(z, o):
        to = 2 * lax.rem(y + o, n_y) + c
        return rcopy(
            y2s.at[z - n_z1, o - 1], y2r.at[z - n_z1, o - 1],
            r2s.at[z, o - 1], r2r.at[z, o - 1], (v, to),
        )

    def after_core(z):
        core_copy(z).wait_recv()
        if z < n_z1:
            for o in range(1, n_y):
                to = lax.rem(y + o, n_y)
                for pp in range(2):
                    y1s[z, o - 1, pp] = (
                        mine[z, pp, to] + core_in[z, pp, to].astype(jnp.float32)
                    ).astype(jnp.bfloat16)
                launch(y1_copy(z, o))
        else:
            for yy in range(n_y):
                x2s[z - n_z1, yy] = (
                    mine[z, 1 - p, yy] + core_in[z, 1 - p, yy].astype(jnp.float32)
                ).astype(jnp.bfloat16)
            launch(x2_copy(z))

    def after_first(z):
        if z < n_z1:
            for o in range(1, n_y):
                y1_copy(z, o).wait_recv()

            def total(which):
                out = mine[z, which, y] + core_in[z, which, y].astype(jnp.float32)
                for o in range(1, n_y):
                    out += y1r[z, o - 1, which].astype(jnp.float32)
                return out

            x1s[z] = total(1 - p).astype(jnp.bfloat16)
            launch(x1_copy(z))
            zf[z] = total(p)
        else:
            x2_copy(z).wait_recv()

            def total(yy):
                return (
                    mine[z, p, yy] + core_in[z, p, yy].astype(jnp.float32)
                    + x2r[z - n_z1, yy].astype(jnp.float32)
                )

            for o in range(1, n_y):
                y2s[z - n_z1, o - 1] = total(lax.rem(y + o, n_y)).astype(jnp.bfloat16)
                launch(y2_copy(z, o))
            zf[z] = total(y)

    def z_copy(z):
        return rcopy(zs.at[z], zr.at[q], z_ss.at[z], z_rs.at[q], (2 * z + p, d))

    def after_second(z):
        if z < n_z1:
            x1_copy(z).wait_recv()
            full = zf[z] + x1r[z].astype(jnp.float32)
        else:
            full = zf[z]
            for o in range(1, n_y):
                y2_copy(z, o).wait_recv()
                full += y2r[z - n_z1, o - 1].astype(jnp.float32)
        zf[z] = full
        zs[z] = full.astype(jnp.bfloat16)

        @pl.when(q != z)
        def _():
            z_copy(z).start()

    n_gw = sh.shape[1] // 512
    gw_copies = []

    def weight_part(b):
        sl = pl.ds(b * 512, 512)
        gw_buf[:, sl] = jnp.dot(
            grad[...], sh[:, sl], preferred_element_type=jnp.float32
        ).astype(jnp.bfloat16)
        cp = pltpu.make_async_copy(gw_buf.at[:, sl], gw_out.at[:, sl], gw_sem.at[b])
        cp.start()
        gw_copies.append(cp)

    for z in order:
        hidden_part(z)
        launch(core_copy(z))
    for z in order:
        after_core(z)
    for b in range(n_gw):
        weight_part(b)
    for z in order:
        after_first(z)
    for z in order:
        after_second(z)
    zf_q = zf[q]
    mine_sum = [zf_q]
    total = zf_q
    for o in range(1, n_z):
        src = lax.rem(q + o, n_z)
        rcopy(zs.at[src], zr.at[src], z_ss.at[src], z_rs.at[src], (v_pair, d)).wait_recv()
        total += zr[src].astype(jnp.float32)
    gh_out[...] = total.astype(jnp.bfloat16)

    for cp in sends + loss_copies + mate_copies:
        cp.wait_send()
    for o in range(1, n_z):
        dst = lax.rem(q + o, n_z)
        rcopy(zs.at[dst], zr.at[q], z_ss.at[dst], z_rs.at[q], (2 * dst + p, d)).wait_send()
    for cp in gw_copies:
        cp.wait()


def hand_over(kl, gh, gw):
    parts = 4
    step = gw.shape[0] // parts

    def move(kl_in, gh_in, gw_in, kl_to, gh_to, gw_to, kl_v, gh_v, gw_v, sem_in, sem_out):
        plan = [(kl_in, kl_v, kl_to), (gh_in, gh_v, gh_to)]
        for i in range(parts):
            sl = pl.ds(i * step, step)
            plan.append((gw_in.at[sl], gw_v.at[sl], gw_to.at[sl]))
        reads = [pltpu.make_async_copy(a, b, sem_in.at[i]) for i, (a, b, _) in enumerate(plan)]
        writes = [pltpu.make_async_copy(b, e, sem_out.at[i]) for i, (_, b, e) in enumerate(plan)]
        for cp in reads:
            cp.start()
        for cp, out in zip(reads, writes):
            cp.wait()
            out.start()
        for out in writes:
            out.wait()

    spec = pl.BlockSpec(memory_space=pl.ANY)
    arrays = (kl, gh, gw)
    return pl.pallas_call(
        move,
        out_shape=tuple(jax.ShapeDtypeStruct(a.shape, a.dtype) for a in arrays),
        in_specs=[spec] * 3,
        out_specs=(spec,) * 3,
        scratch_shapes=[pltpu.VMEM(a.shape, a.dtype) for a in arrays]
        + [pltpu.SemaphoreType.DMA((parts + 2,))] * 2,
        name="hand_over",
    )(*arrays)


def solution(mesh):
    n_vocab, n_dp = mesh.shape["vocab"], mesh.shape["dp"]

    def local(th_own, sh_own, codes, scales, weight, loss_scale):
        tok, dt = th_own.shape
        ds_ = sh_own.shape[1]
        rows = codes.shape[0]
        n_tok = tok * n_dp
        n_y, n_z = n_dp // 2, n_vocab // 2
        n_off, n_z1 = n_y - 1, n_z // 2
        n_z2 = n_z - n_z1
        rv = ds_ // n_vocab
        n_ch = dt // step_width(dt) + ds_ // step_width(ds_)
        n_a, n_b = 2 * n_dp - 1, n_z - 1
        bf, f32 = jnp.bfloat16, jnp.float32
        V, D = pltpu.VMEM, pltpu.SemaphoreType.DMA
        any_spec = pl.BlockSpec(memory_space=pl.ANY)
        vm_spec = pl.BlockSpec(memory_space=pltpu.VMEM)
        kl, gh, gw = pl.pallas_call(
            functools.partial(kernel, n_vocab, n_dp),
            out_shape=(
                jax.ShapeDtypeStruct((1, tok), f32),
                jax.ShapeDtypeStruct((rv, tok), bf),
                jax.ShapeDtypeStruct((rows, ds_), bf),
            ),
            in_specs=[any_spec, any_spec, any_spec, vm_spec, any_spec, vm_spec],
            out_specs=(vm_spec, vm_spec, any_spec),
            scratch_shapes=[
                V((n_tok, dt), bf), V((n_tok, ds_), bf), V((rows, dt), bf), V((rows, ds_), bf),
                V((ds_, rows), bf), V((rows, n_tok), f32), V((rows, n_tok), f32),
                V((n_dp, 8, tok), f32), V((8, n_tok), f32), V((8, n_tok), f32),
                V((8, n_tok), f32), V((n_a, 8, n_tok), f32), V((n_b, 8, n_tok), f32),
                V((rows, n_tok), bf), V((rows, ds_), bf),
                V((n_z, 2, n_y, rv, tok), f32), V((n_z, 2, n_y, rv, tok), bf),
                V((n_z, 2, n_y, rv, tok), bf),
                V((n_z1, n_off, 2, rv, tok), bf), V((n_z1, n_off, 2, rv, tok), bf),
                V((n_z1, rv, tok), bf), V((n_z1, rv, tok), bf),
                V((n_z2, n_y, rv, tok), bf), V((n_z2, n_y, rv, tok), bf),
                V((n_z2, n_off, rv, tok), bf), V((n_z2, n_off, rv, tok), bf),
                V((n_z, rv, tok), bf), V((n_z, rv, tok), bf), V((n_z, rv, tok), f32),
                V((rows, -(-scales.shape[1] // 8) * 8), f32), V((8, tok), f32),
                D((n_ch + 2,)), D((ds_ // 512,)), D((2,)), D((2,)),
                D((10, n_off, n_ch)), D((10, n_off, n_ch)),
                D((n_dp - 1,)), D((n_dp - 1,)), D((n_a,)), D((n_a,)), D((n_b,)), D((n_b,)),
                D((n_z,)), D((n_z,)), *[D((n_z, n_off))] * 4, D((n_z,)), D((n_z,)),
            ],
            compiler_params=pltpu.CompilerParams(
                collective_id=0, has_side_effects=True, vmem_limit_bytes=60 * 1024 * 1024
            ),
            name="distill",
        )(th_own, sh_own, codes, scales.T, weight, loss_scale)
        kl, gh, gw = hand_over(kl, gh, gw)
        return kl.reshape(tok), gh.T, gw

    in_specs = (
        P("dp", None),
        P("dp", None),
        P(("vocab", "dp"), None),
        P(("vocab", "dp"), None),
        P(("vocab", "dp"), None),
        P("dp"),
    )
    out_specs = (P("dp"), P("dp", "vocab"), P(("vocab", "dp"), None))
    return jax.shard_map(local, mesh=mesh, in_specs=in_specs, out_specs=out_specs, check_vma=False)
```

profile of v0, /device:TPU:1, one launch (start us, length us, event | category | flops | bytes accessed | tf_op | source)
XLA Modules:
  0.0 66.0 jit_solution(2281199547502548004)
XLA Ops:
  0.6 62.7 %distill.1 = (f32[1,128]{1,0:T(1,128)}, bf16[320,128]{1,0:T(8,128)(2,1)}, bf16[512,2560]{1,0:T(8,128)(2,1)}) custom-call(bf16[128,5376]{1,0:T(8,128)(2,1)} %th_own.1, bf16[128,2560]{1,0:T(8,128)(2,1)} %sh_own.1, bf16[512,5376]{1,0:T(8,128)(2,1)} %codes.1, f32[42,512]{1,0:T(8,128)} %bitcast.3, bf16[512,2560]{1,0:T(8,128)(2,1)} %weight.1, bf16[128]{0:T(256)(128)(2,1)} %loss_in.1), custom_call_target="tpu_custom_call" | custom-call | tf_op jit(solution)/shard_map/distill/pallas_call | solution.py:517
  63.3 2.7 %hand_over.1 = (f32[1,128]{1,0:T(1,128)}, bf16[320,128]{1,0:T(8,128)(2,1)}, bf16[512,2560]{1,0:T(8,128)(2,1)}) custom-call(f32[1,128]{1,0:T(1,128)} %get-tuple-element.9.kl_in, bf16[320,128]{1,0:T(8,128)(2,1)} %get-tuple-element.10.gh_in, bf16[512,2560]{1,0:T(8,128)(2,1)} %get-tuple-element.11.gw_in), custom_call_target="tpu_custom_call" | custom-call | tf_op jit(solution)/shard_map/hand_over/pallas_call | solution.py:488
where the time goes:
time: 67.3 us; the launch traced here: 66 us
  Pallas kernels  65.4 us (97%)
    pallas_call x1, Pallas kernels, local(): pl.pallas_call(functools.partial(kernel, n_vocab, n_dp), out_shape=(jax.S...  62.7 us
    pallas_call x1, Pallas kernels, hand_over(): pl.pallas_call(move, out_shape=tuple((jax.ShapeDtypeStruct(a.shape, a.dty...  2.73 us

commit v1 on v0

v1 whole, which is shorter than its diff:
```python
import functools

import jax
import jax.numpy as jnp
from jax import lax
from jax.experimental import pallas as pl
from jax.experimental.pallas import tpu as pltpu
from jax.sharding import PartitionSpec as P

GROUP = 128
LANE = 128
MESH = pl.DeviceIdType.MESH

PLAY_A = (
    "s1", "s2", "s3", "s4", "s5", "p0", "q0", "p1", "q1", "p2",
)
PLAY_B = (
    "y0", "q2", "y1", "p3", "y2", "x0", "q3", "y3", "x1", "y4", "f0", "00", "y5", "x2", "p4",
    "p5", "x3", "f1", "01", "x4", "f2", "02", "x5", "f3", "03", "f4", "04", "f5", "05",
)
PLAY_C = (
    "d0", "m0", "10", "d1", "m1", "11",
)
PLAY_D = (
    "p0", "q0", "p1", "q1", "p2", "q2", "p3", "q3", "d0", "d1", "s0", "p4", "d2", "s1", "p5",
)
PLAY_E = (
    "d3", "s2", "s3", "s4", "s5",
)
PLAY_F = (
    "m0", "00", "y0", "y1", "m1", "01", "y2", "x0", "m2", "02", "y3", "x1", "m3", "03", "y4",
    "f0", "m4", "04", "y5", "x2", "m5", "05",
)
PLAY_G = (
    "f1", "x3", "10", "f2", "11", "x4",
)
PLAY_H = (
    "f3", "12", "x5", "f4", "13", "f5",
)


def dot_t(left_rows, right_rows):
    return lax.dot_general(
        left_rows, right_rows, (((1,), (1,)), ((), ())), preferred_element_type=jnp.float32
    )


def chunk_widths(cols, lead):
    units = cols // 256
    head = [3] if lead and units > 3 else []
    rest = units - sum(head)
    per = max(k for k in (1, 2, 3, 5, 6, 7) if rest % k == 0)
    return [256 * n for n in head + [per] * (rest // per)]


def kernel(
    n_vocab, n_dp,
    th_own, sh_own, codes, scales, weight, loss_in,
    kl_out, gh_out, gw_out,
    th, sh, table, wgt, wgt_t, tlog, slog, lsc, stat, stat_b, fin, in_a, in_b,
    grad, gw_buf, mine, theirs, core_in,
    y1s, y1r, x1s, x1r, x2s, x2r, y2s, y2r, zs, zr, zf,
    sc_rows, loss_row, ld_sem, gw_sem, pc_s, pc_r, hop_s, hop_r,
    ls_s, ls_r, a_s, a_r, b_s, b_r, cs, cr, r1s, r1r, r2s, r2r, z_ss, z_rs,
):
    v, d = lax.axis_index("vocab"), lax.axis_index("dp")
    core, y = lax.rem(d, 2), lax.div(d, 2)
    p, q = lax.rem(v, 2), lax.div(v, 2)
    n_y, n_z = n_dp // 2, n_vocab // 2
    v_pair = 2 * q + 1 - p
    r = lax.rem(q, 2)
    v_quad = 2 * (q + 1 - 2 * r) + p
    tok = th_own.shape[0]
    rv = zr.shape[1]
    n_z1 = n_z // 2
    span = n_y * tok
    quarter = tok // 4

    def rcopy(src, dst, send, recv, dev):
        return pltpu.make_async_remote_copy(
            src_ref=src, dst_ref=dst, send_sem=send, recv_sem=recv,
            device_id=dev, device_id_type=MESH,
        )

    peers_a = []
    for dv in range(2):
        for dd in range(n_dp):
            if dv or dd:
                peers_a.append((v if dv == 0 else v_pair, lax.rem(d + dd, n_dp)))
    peers_b = [(2 * lax.rem(q + o, n_z) + p, d) for o in range(1, n_z)]
    barrier = pltpu.get_barrier_semaphore()
    for peer in peers_a + peers_b:
        pl.semaphore_signal(barrier, inc=1, device_id=peer, device_id_type=MESH)

    chunks = []
    for own, scr, tab, acc in ((th_own, th, table, tlog), (sh_own, sh, wgt, slog)):
        base = 0
        for width in chunk_widths(own.shape[1], tab is table):
            chunks.append((own, scr, tab, acc, base, width))
            base += width
    n_ch = len(chunks)
    firsts = [k == 0 or chunks[k][3] is not chunks[k - 1][3] for k in range(n_ch)]
    by_y = [False] * n_ch
    room = sum(ch[5] for ch in chunks) * 55 // 100
    for k in reversed(range(n_ch)):
        room -= chunks[k][5]
        if room < 0:
            break
        by_y[k] = True

    def block(g, yy):
        return pl.multiple_of((g * n_y + yy) * tok, tok)

    my_rows = pl.ds(pl.multiple_of((core * n_y + y) * tok, tok), tok)
    loads = []
    for k, (own, scr, tab, acc, base, width) in enumerate(chunks):
        src = codes if tab is table else weight
        cp = pltpu.make_async_copy(
            src.at[:, pl.ds(base, width)], tab.at[:, pl.ds(base, width)], ld_sem.at[k]
        )
        cp.start()
        loads.append(cp)
    own_loads = [
        pltpu.make_async_copy(th_own, th.at[my_rows], ld_sem.at[n_ch]),
        pltpu.make_async_copy(sh_own, sh.at[my_rows], ld_sem.at[n_ch + 1]),
    ]
    for cp in own_loads:
        cp.start()
    groups = scales.shape[0]
    pad = jnp.zeros((sc_rows.shape[1] - groups, LANE), jnp.float32)
    for b in range(0, scales.shape[1], LANE):
        sc_rows[pl.ds(b, LANE), :] = jnp.concatenate(
            [scales[:, pl.ds(b, LANE)], pad], axis=0
        ).T
    loss_row[...] = jnp.broadcast_to(
        loss_in[...].astype(jnp.float32).reshape(1, tok), loss_row.shape
    )
    lsc[core * n_y + y] = loss_row[...]
    with jax.named_scope("barrier"):
        pl.semaphore_wait(barrier, len(peers_a) + len(peers_b))

    A, B, C, E = 2 * r + p, 2 * r + 1 - p, 2 * (1 - r) + p, 2 * (1 - r) + 1 - p
    Y_A, Y_E, X_A, Z_A, X_C, Z_B, D_A, D_B, D_C, D_E = range(10)
    order = []
    for i in range(n_z1):
        order += [i, n_z1 + i]
    order += [i for i in range(n_z) if i not in order]
    n_gw = sh.shape[1] // 512

    def run(c):
        mate = 2 * y + 1 - c
        X, Z = (v_pair, d), (v_quad, d)
        sends = []
        gw_copies = []

        def launch(cp):
            cp.start()
            sends.append(cp)

        def region(g, k, yy, piece, half=None):
            scr, base, width = chunks[k][1], chunks[k][4], chunks[k][5]
            first, size = block(g, yy) + piece * quarter, quarter
            if half is not None:
                size = quarter // 2
                first += half * size
            return scr.at[pl.ds(pl.multiple_of(first, size), size), pl.ds(base, width)]

        def came(o):
            return lax.rem(y + n_y - o, n_y)

        def y_send(k, kind):
            own, base, width = chunks[k][0], chunks[k][4], chunks[k][5]
            piece = A if kind == Y_A else E
            src = own.at[
                pl.ds(pl.multiple_of(piece * quarter, quarter), quarter), pl.ds(base, width)
            ]
            for o in range(1, n_y):
                to = 2 * lax.rem(y + o, n_y) + c
                launch(rcopy(
                    src, region(c, k, y, piece),
                    hop_s.at[kind, o - 1, k], hop_r.at[kind, o - 1, k], (v, to),
                ))

        def hop(kind, k, o, g, piece, dev, half=None):
            ref = region(g, k, came(o), piece, half)
            return rcopy(ref, ref, hop_s.at[kind, o - 1, k], hop_r.at[kind, o - 1, k], dev)

        def to_mate(kind, k, o, piece):
            launch(hop(kind, k, o, c, piece, (v, mate)))

        def stage_y(k):
            for o in range(1, n_y):
                hop(Y_A, k, o, c, A, X).wait_recv()
                launch(hop(X_A, k, o, c, A, X))
                launch(hop(Z_A, k, o, c, A, Z))
                to_mate(D_A, k, o, A)

        def stage_xz(k):
            for o in range(1, n_y):
                hop(X_A, k, o, c, B, X).wait_recv()
                if not by_y[k]:
                    launch(hop(Z_B, k, o, c, B, Z, 1))
                to_mate(D_B, k, o, B)
                hop(Z_A, k, o, c, C, Z).wait_recv()
                if not by_y[k]:
                    launch(hop(X_C, k, o, c, C, X, 0))
                to_mate(D_C, k, o, C)

        def stage_far(k):
            for o in range(1, n_y):
                if by_y[k]:
                    hop(Y_E, k, o, c, E, X).wait_recv()
                else:
                    hop(X_C, k, o, c, E, X, 0).wait_recv()
                    hop(Z_B, k, o, c, E, Z, 1).wait_recv()
                to_mate(D_E, k, o, E)

        def mate_wait(k, pairs):
            for o in range(1, n_y):
                for kind, piece in pairs:
                    hop(kind, k, o, 1 - c, piece, X).wait_recv()

        first_pair = [(D_A, A)]
        rest_pairs = [(D_B, B), (D_C, C), (D_E, E)]

        def prepare(k, half):
            own, scr, tab, acc, base, width = chunks[k]
            if half == 0:
                loads[k].wait()
            steps = table.shape[0] // 128
            if tab is table:
                @pl.loop(half * steps, (half + 1) * steps)
                def _(i):
                    rsl = pl.ds(pl.multiple_of(i * 64, 64), 64)
                    sc = sc_rows[rsl, :]
                    for g in range(width // GROUP):
                        lane = pl.ds(base + g * GROUP, GROUP)
                        col = (base + g * GROUP) // GROUP
                        wide = table[rsl, lane].astype(jnp.float32) * sc[:, col : col + 1]
                        table[rsl, lane] = wide.astype(jnp.bfloat16)
            elif half == 0:
                for b in range(base, base + width, 256):
                    wgt_t[pl.ds(b, 256), :] = wgt[:, pl.ds(b, 256)].T

        def product(g, k):
            own, scr, tab, acc, base, width = chunks[k]
            for b in range(g * span, (g + 1) * span, 2 * tok):
                two = pl.ds(b, 2 * tok)
                part = dot_t(tab[:, pl.ds(base, width)], scr[two, pl.ds(base, width)])
                if firsts[k]:
                    acc[:, two] = part
                else:
                    acc[:, two] += part

        def local_stat(g):
            @pl.loop(0, n_y)
            def _(j):
                off = pl.multiple_of(j * tok, tok)
                sl = pl.ds(pl.multiple_of(g * span + j * tok, tok), tok)
                t_max = jnp.max(tlog[:, sl], axis=0, keepdims=True)
                s_max = jnp.max(slog[:, sl], axis=0, keepdims=True)
                te = jnp.exp(tlog[:, sl] - t_max)
                t_sum = jnp.sum(te, axis=0, keepdims=True)
                x_sum = jnp.sum(te * (tlog[:, sl] - slog[:, sl]), axis=0, keepdims=True)
                tlog[:, sl] = te
                se = jnp.exp(slog[:, sl] - s_max)
                s_sum = jnp.sum(se, axis=0, keepdims=True)
                slog[:, sl] = se
                stat[g, :, pl.ds(off, tok)] = jnp.concatenate(
                    [t_max, t_sum, x_sum, s_max, s_sum, jnp.zeros((3, tok), jnp.float32)],
                    axis=0,
                )

        def merge(parts):
            t_top = functools.reduce(jnp.maximum, [x[0:1] for x in parts])
            s_top = functools.reduce(jnp.maximum, [x[3:4] for x in parts])
            t_sum = x_sum = s_sum = 0.0
            for x in parts:
                t_w = jnp.exp(x[0:1] - t_top)
                t_sum += x[1:2] * t_w
                x_sum += x[2:3] * t_w
                s_sum += x[4:5] * jnp.exp(x[3:4] - s_top)
            return t_top, t_sum, x_sum, s_top, s_sum

        def a_copy(g, i):
            return rcopy(stat.at[g], in_a.at[g, i], a_s.at[g, i], a_r.at[g, i], peers_a[i])

        def b_copy(g, i):
            return rcopy(stat_b.at[g], in_b.at[g, i], b_s.at[g, i], b_r.at[g, i], peers_b[i])

        def send_a(g):
            local_stat(g)
            for i in reversed(range(len(peers_a))):
                launch(a_copy(g, i))

        def send_b(g):
            for i in range(len(peers_a)):
                a_copy(g, i).wait_recv()
            stat_b[g] = jnp.concatenate(
                list(merge([stat[g]] + [in_a[g, i] for i in range(len(peers_a))]))
                + [jnp.zeros((3, span), jnp.float32)], axis=0
            )
            for i in range(len(peers_b)):
                launch(b_copy(g, i))

        def finish(g):
            for i in range(len(peers_b)):
                b_copy(g, i).wait_recv()
            t_top, t_sum, x_sum, s_top, s_sum = merge(
                [stat_b[g]] + [in_b[g, i] for i in range(len(peers_b))]
            )
            t_lse = t_top + jnp.log(t_sum)
            s_lse = s_top + jnp.log(s_sum)
            fin[g] = jnp.concatenate(
                [
                    x_sum / t_sum - t_lse + s_lse,
                    jnp.exp(stat[g, 0:1] - t_lse),
                    jnp.exp(stat[g, 3:4] - s_lse),
                    jnp.zeros((5, span), jnp.float32),
                ],
                axis=0,
            )
            if g == c:
                kl_out[...] = fin[g, 0:1, pl.ds(pl.multiple_of(y * tok, tok), tok)]

            @pl.loop(0, n_y)
            def _(j):
                off = pl.multiple_of(j * tok, tok)
                sl = pl.ds(pl.multiple_of(g * span + j * tok, tok), tok)
                f = fin[g, :, pl.ds(off, tok)]
                grad[:, sl] = (
                    lsc[g * n_y + j][0:1] * (slog[:, sl] * f[2:3] - tlog[:, sl] * f[1:2])
                ).astype(jnp.bfloat16)

        def hidden(g, z):
            for pp in range(2):
                feat = wgt_t[pl.ds((2 * z + pp) * rv, rv), :]
                for yy in range(0, n_y, 2):
                    part = jnp.dot(
                        feat, grad[:, pl.ds(g * span + yy * tok, 2 * tok)],
                        preferred_element_type=jnp.float32,
                    )
                    for h in range(2):
                        one = part[:, h * tok : (h + 1) * tok]
                        if g == c:
                            mine[z, pp, yy + h] = one
                        else:
                            theirs[z, pp, yy + h] = one.astype(jnp.bfloat16)
            if g != c:
                launch(core_copy(z))

        def core_copy(z):
            return rcopy(theirs.at[z], core_in.at[z], cs.at[z], cr.at[z], (v, mate))

        def y1_copy(z, o):
            to = 2 * lax.rem(y + o, n_y) + c
            return rcopy(
                y1s.at[z, o - 1], y1r.at[z, o - 1], r1s.at[z, o - 1], r1r.at[z, o - 1], (v, to)
            )

        def x1_copy(z):
            return rcopy(x1s.at[z], x1r.at[z], r2s.at[z, 0], r2r.at[z, 0], (v_pair, d))

        def x2_copy(z):
            return rcopy(
                x2s.at[z - n_z1], x2r.at[z - n_z1], r1s.at[z, 0], r1r.at[z, 0], (v_pair, d)
            )

        def y2_copy(z, o):
            to = 2 * lax.rem(y + o, n_y) + c
            return rcopy(
                y2s.at[z - n_z1, o - 1], y2r.at[z - n_z1, o - 1],
                r2s.at[z, o - 1], r2r.at[z, o - 1], (v, to),
            )

        def after_core(z):
            core_copy(z).wait_recv()
            if z < n_z1:
                for o in range(1, n_y):
                    to = lax.rem(y + o, n_y)
                    for pp in range(2):
                        y1s[z, o - 1, pp] = (
                            mine[z, pp, to] + core_in[z, pp, to].astype(jnp.float32)
                        ).astype(jnp.bfloat16)
                    launch(y1_copy(z, o))
            else:
                for yy in range(n_y):
                    x2s[z - n_z1, yy] = (
                        mine[z, 1 - p, yy] + core_in[z, 1 - p, yy].astype(jnp.float32)
                    ).astype(jnp.bfloat16)
                launch(x2_copy(z))

        def after_first(z):
            if z < n_z1:
                for o in range(1, n_y):
                    y1_copy(z, o).wait_recv()

                def total(which):
                    out = mine[z, which, y] + core_in[z, which, y].astype(jnp.float32)
                    for o in range(1, n_y):
                        out += y1r[z, o - 1, which].astype(jnp.float32)
                    return out

                x1s[z] = total(1 - p).astype(jnp.bfloat16)
                launch(x1_copy(z))
                zf[z] = total(p)
            else:
                x2_copy(z).wait_recv()

                def total(yy):
                    return (
                        mine[z, p, yy] + core_in[z, p, yy].astype(jnp.float32)
                        + x2r[z - n_z1, yy].astype(jnp.float32)
                    )

                for o in range(1, n_y):
                    y2s[z - n_z1, o - 1] = total(lax.rem(y + o, n_y)).astype(jnp.bfloat16)
                    launch(y2_copy(z, o))
                zf[z] = total(y)

        def z_copy(z):
            return rcopy(zs.at[z], zr.at[q], z_ss.at[z], z_rs.at[q], (2 * z + p, d))

        def after_second(z):
            if z < n_z1:
                x1_copy(z).wait_recv()
                full = zf[z] + x1r[z].astype(jnp.float32)
            else:
                full = zf[z]
                for o in range(1, n_y):
                    y2_copy(z, o).wait_recv()
                    full += y2r[z - n_z1, o - 1].astype(jnp.float32)
            zf[z] = full
            zs[z] = full.astype(jnp.bfloat16)

            @pl.when(q != z)
            def _():
                z_copy(z).start()

        def weight_part(b):
            sl = pl.ds(b * 512, 512)
            gw_buf[:, sl] = jnp.dot(
                grad[...], sh[:, sl], preferred_element_type=jnp.float32
            ).astype(jnp.bfloat16)
            cp = pltpu.make_async_copy(gw_buf.at[:, sl], gw_out.at[:, sl], gw_sem.at[b])
            cp.start()
            gw_copies.append(cp)

        def last():
            total = zf[q]
            for o in range(1, n_z):
                src = lax.rem(q + o, n_z)
                rcopy(
                    zs.at[src], zr.at[src], z_ss.at[src], z_rs.at[src], (v_pair, d)
                ).wait_recv()
                total += zr[src].astype(jnp.float32)
            gh_out[...] = total.astype(jnp.bfloat16)

        def loss_wait():
            for dd in range(1, n_dp):
                other = lax.rem(d + n_dp - dd, n_dp)
                slot = lax.rem(other, 2) * n_y + lax.div(other, 2)
                rcopy(
                    loss_row, lsc.at[slot], ls_s.at[dd - 1], ls_r.at[dd - 1], (v, mate)
                ).wait_recv()

        def mate_copies():
            for i, (own, scr) in enumerate(((th_own, th), (sh_own, sh))):
                launch(rcopy(
                    own, scr.at[pl.ds(block(c, y), tok)], pc_s.at[i], pc_r.at[i], (v, mate)
                ))

        def mate_arrived():
            for i, (own, scr) in enumerate(((th_own, th), (sh_own, sh))):
                rcopy(
                    own, scr.at[pl.ds(block(1 - c, y), tok)], pc_s.at[i], pc_r.at[i], (v, mate)
                ).wait_recv()

        def named(name, fn, *args):
            with jax.named_scope(name + "_".join(str(x) for x in args if isinstance(x, int))):
                fn(*args)

        for dd in range(1, n_dp):
            launch(rcopy(
                loss_row, lsc.at[c * n_y + y], ls_s.at[dd - 1], ls_r.at[dd - 1],
                (v, lax.rem(d + dd, n_dp)),
            ))
        far = [k for k in range(n_ch) if by_y[k]]

        def send_y(k):
            y_send(k, Y_A)
            if k == n_ch - 1:
                for kk in far:
                    y_send(kk, Y_E)

        ops = {
            "p": lambda k: prepare(k, 0),
            "q": lambda k: prepare(k, 1),
            "s": send_y,
            "y": stage_y,
            "x": stage_xz,
            "f": stage_far,
            "d": lambda k: mate_wait(k, first_pair),
            "m": lambda k: mate_wait(k, rest_pairs),
            "0": lambda k: product(0, k),
            "1": lambda k: product(1, k),
        }
        done = set()

        def play(steps, flush):
            todo = [(step[0], int(step[1:])) for step in steps]
            todo += [(name, k) for k in range(n_ch) for name in flush]
            for name, k in todo:
                if k < n_ch and (name, k) not in done:
                    done.add((name, k))
                    named(name, ops[name], k)

        if c == 0:
            play(("s0",), "")
            mate_copies()
            play(PLAY_A, "")
            for cp in own_loads:
                cp.wait()
            play(PLAY_B, "spqyxf0")
            named("send_a", send_a, 0)
            named("mate_arrived", mate_arrived)
            play(PLAY_C, "")
            named("send_b", send_b, 0)
            play((), "dm1")
            named("send_a", send_a, 1)
            loss_wait()
            named("finish", finish, 0)
            for i, z in enumerate(order):
                named("hidden", hidden, 0, z)
                if i >= 1:
                    named("after_core", after_core, order[i - 1])
            named("after_core", after_core, order[-1])
            named("send_b", send_b, 1)
            named("finish", finish, 1)
            for z in order:
                named("hidden", hidden, 1, z)
            for z in order:
                named("after_first", after_first, z)
            for b in range(n_gw):
                named("weight", weight_part, b)
            for z in order:
                named("after_second", after_second, z)
            named("last", last)
        else:
            mate_copies()
            play(PLAY_D, "pq")
            for cp in own_loads:
                cp.wait()
            play(PLAY_E, "ds")
            named("mate_arrived", mate_arrived)
            play(PLAY_F, "m0")
            named("send_a", send_a, 0)
            play(PLAY_G, "")
            named("send_b", send_b, 0)
            play(PLAY_H, "yxf1")
            named("send_a", send_a, 1)
            loss_wait()
            named("finish", finish, 0)
            for z in order:
                named("hidden", hidden, 0, z)
            named("send_b", send_b, 1)
            named("finish", finish, 1)
            for i, z in enumerate(order):
                named("hidden", hidden, 1, z)
                if i >= 1:
                    named("after_core", after_core, order[i - 1])
            named("after_core", after_core, order[-1])
            for b in range(n_gw):
                named("weight", weight_part, b)
            for z in order:
                named("after_first", after_first, z)
            for z in order:
                named("after_second", after_second, z)
            named("last", last)

        for cp in sends:
            cp.wait_send()
        for o in range(1, n_z):
            dst = lax.rem(q + o, n_z)
            rcopy(zs.at[dst], zr.at[q], z_ss.at[dst], z_rs.at[q], (2 * dst + p, d)).wait_send()
        for cp in gw_copies:
            cp.wait()

    for which in range(2):
        pl.when(core == which)(functools.partial(run, which))


def hand_over(kl, gh, gw):
    parts = 4
    step = gw.shape[0] // parts

    def move(kl_in, gh_in, gw_in, kl_to, gh_to, gw_to, kl_v, gh_v, gw_v, sem_in, sem_out):
        plan = [(kl_in, kl_v, kl_to), (gh_in, gh_v, gh_to)]
        for i in range(parts):
            sl = pl.ds(i * step, step)
            plan.append((gw_in.at[sl], gw_v.at[sl], gw_to.at[sl]))
        reads = [pltpu.make_async_copy(a, b, sem_in.at[i]) for i, (a, b, _) in enumerate(plan)]
        writes = [pltpu.make_async_copy(b, e, sem_out.at[i]) for i, (_, b, e) in enumerate(plan)]
        for cp in reads:
            cp.start()
        for cp, out in zip(reads, writes):
            cp.wait()
            out.start()
        for out in writes:
            out.wait()

    spec = pl.BlockSpec(memory_space=pl.ANY)
    arrays = (kl, gh, gw)
    return pl.pallas_call(
        move,
        out_shape=tuple(jax.ShapeDtypeStruct(a.shape, a.dtype) for a in arrays),
        in_specs=[spec] * 3,
        out_specs=(spec,) * 3,
        scratch_shapes=[pltpu.VMEM(a.shape, a.dtype) for a in arrays]
        + [pltpu.SemaphoreType.DMA((parts + 2,))] * 2,
        name="hand_over",
    )(*arrays)


def solution(mesh):
    n_vocab, n_dp = mesh.shape["vocab"], mesh.shape["dp"]

    def local(th_own, sh_own, codes, scales, weight, loss_scale):
        tok, dt = th_own.shape
        ds_ = sh_own.shape[1]
        rows = codes.shape[0]
        n_tok = tok * n_dp
        n_y, n_z = n_dp // 2, n_vocab // 2
        n_off, n_z1 = n_y - 1, n_z // 2
        n_z2 = n_z - n_z1
        rv = ds_ // n_vocab
        n_ch = len(chunk_widths(dt, True)) + len(chunk_widths(ds_, False))
        span = n_y * tok
        n_a, n_b = 2 * n_dp - 1, n_z - 1
        bf, f32 = jnp.bfloat16, jnp.float32
        V, D = pltpu.VMEM, pltpu.SemaphoreType.DMA
        any_spec = pl.BlockSpec(memory_space=pl.ANY)
        vm_spec = pl.BlockSpec(memory_space=pltpu.VMEM)
        kl, gh, gw = pl.pallas_call(
            functools.partial(kernel, n_vocab, n_dp),
            out_shape=(
                jax.ShapeDtypeStruct((1, tok), f32),
                jax.ShapeDtypeStruct((rv, tok), bf),
                jax.ShapeDtypeStruct((rows, ds_), bf),
            ),
            in_specs=[any_spec, any_spec, any_spec, vm_spec, any_spec, vm_spec],
            out_specs=(vm_spec, vm_spec, any_spec),
            scratch_shapes=[
                V((n_tok, dt), bf), V((n_tok, ds_), bf), V((rows, dt), bf), V((rows, ds_), bf),
                V((ds_, rows), bf), V((rows, n_tok), f32), V((rows, n_tok), f32),
                V((n_dp, 8, tok), f32), V((2, 8, span), f32), V((2, 8, span), f32),
                V((2, 8, span), f32), V((2, n_a, 8, span), f32), V((2, n_b, 8, span), f32),
                V((rows, n_tok), bf), V((rows, ds_), bf),
                V((n_z, 2, n_y, rv, tok), f32), V((n_z, 2, n_y, rv, tok), bf),
                V((n_z, 2, n_y, rv, tok), bf),
                V((n_z1, n_off, 2, rv, tok), bf), V((n_z1, n_off, 2, rv, tok), bf),
                V((n_z1, rv, tok), bf), V((n_z1, rv, tok), bf),
                V((n_z2, n_y, rv, tok), bf), V((n_z2, n_y, rv, tok), bf),
                V((n_z2, n_off, rv, tok), bf), V((n_z2, n_off, rv, tok), bf),
                V((n_z, rv, tok), bf), V((n_z, rv, tok), bf), V((n_z, rv, tok), f32),
                V((rows, -(-scales.shape[1] // 8) * 8), f32), V((8, tok), f32),
                D((n_ch + 2,)), D((ds_ // 512,)), D((2,)), D((2,)),
                D((10, n_off, n_ch)), D((10, n_off, n_ch)),
                D((n_dp - 1,)), D((n_dp - 1,)), *[D((2, n_a))] * 2, *[D((2, n_b))] * 2,
                D((n_z,)), D((n_z,)), *[D((n_z, n_off))] * 4, D((n_z,)), D((n_z,)),
            ],
            compiler_params=pltpu.CompilerParams(
                collective_id=0, has_side_effects=True, vmem_limit_bytes=60 * 1024 * 1024
            ),
            name="distill",
        )(th_own, sh_own, codes, scales.T, weight, loss_scale)
        kl, gh, gw = hand_over(kl, gh, gw)
        return kl.reshape(tok), gh.T, gw

    in_specs = (
        P("dp", None),
        P("dp", None),
        P(("vocab", "dp"), None),
        P(("vocab", "dp"), None),
        P(("vocab", "dp"), None),
        P("dp"),
    )
    out_specs = (P("dp"), P("dp", "vocab"), P(("vocab", "dp"), None))
    return jax.shard_map(local, mesh=mesh, in_specs=in_specs, out_specs=out_specs, check_vma=False)
```

time: 67.3 us -> 60.8 us (0.903); the launches traced: 66 us -> 60.6 us
  Pallas kernels: 65.4 us -> 59.8 us
    pallas_call x1, Pallas kernels: 62.7 us -> 57.1 us  [local(): pl.pallas_call(functools.partial(kernel, n_vocab, n_dp), out_shape=(jax.S...]
where the time goes in v1:
time: 60.8 us; the launch traced here: 60.6 us
  Pallas kernels  59.8 us (98%)
  between operations  0.8 us (1%)
    pallas_call x1, Pallas kernels, local(): pl.pallas_call(functools.partial(kernel, n_vocab, n_dp), out_shape=(jax.S...  57.1 us
    pallas_call x1, Pallas kernels, hand_over(): pl.pallas_call(move, out_shape=tuple((jax.ShapeDtypeStruct(a.shape, a.dty...  2.73 us

profile of v1, /device:TPU:1, one launch (start us, length us, event | category | flops | bytes accessed | tf_op | source)
XLA Modules:
  0.0 60.6 jit_solution(18050642145523666328)
XLA Ops:
  0.6 57.1 %distill.1 = (f32[1,128]{1,0:T(1,128)}, bf16[320,128]{1,0:T(8,128)(2,1)}, bf16[512,2560]{1,0:T(8,128)(2,1)}) custom-call(bf16[128,5376]{1,0:T(8,128)(2,1)} %th_own.1, bf16[128,2560]{1,0:T(8,128)(2,1)} %sh_own.1, bf16[512,5376]{1,0:T(8,128)(2,1)} %codes.1, f32[42,512]{1,0:T(8,128)} %bitcast.3, bf16[512,2560]{1,0:T(8,128)(2,1)} %weight.1, bf16[128]{0:T(256)(128)(2,1)} %loss_in.1), custom_call_target="tpu_custom_call" | custom-call | tf_op jit(solution)/shard_map/distill/pallas_call | solution.py:644
  57.8 2.7 %hand_over.1 = (f32[1,128]{1,0:T(1,128)}, bf16[320,128]{1,0:T(8,128)(2,1)}, bf16[512,2560]{1,0:T(8,128)(2,1)}) custom-call(f32[1,128]{1,0:T(1,128)} %get-tuple-element.9.kl_in, bf16[320,128]{1,0:T(8,128)(2,1)} %get-tuple-element.10.gh_in, bf16[512,2560]{1,0:T(8,128)(2,1)} %get-tuple-element.11.gw_in), custom_call_target="tpu_custom_call" | custom-call | tf_op jit(solution)/shard_map/hand_over/pallas_call | solution.py:614

commit v2 on v1

--- a/solution.py
+++ b/solution.py
@@ -15,27 +15,31 @@
     "s1", "s2", "s3", "s4", "s5", "p0", "q0", "p1", "q1", "p2",
 )
 PLAY_B = (
-    "y0", "q2", "y1", "p3", "y2", "x0", "q3", "y3", "x1", "y4", "f0", "00", "y5", "x2", "p4",
-    "p5", "x3", "f1", "01", "x4", "f2", "02", "x5", "f3", "03", "f4", "04", "f5", "05",
+    "y0", "q2", "y1", "p3", "y2", "q3", "y3", "x0", "y4", "x1", "y5", "p4", "p5", "x2", "f0",
+    "00", "x3", "f1", "01", "x4", "f3", "03", "x5", "f4", "04", "f5", "05", "f2", "02",
 )
 PLAY_C = (
     "d0", "m0", "10", "d1", "m1", "11",
 )
+PLAY_I = (
+    "d3", "m3", "13", "d4", "m4", "14", "d5", "m5", "15",
+)
 PLAY_D = (
-    "p0", "q0", "p1", "q1", "p2", "q2", "p3", "q3", "d0", "d1", "s0", "p4", "d2", "s1", "p5",
+    "p0", "q0", "p1", "q1", "p2", "q2", "p3", "q3", "d0", "s0", "d1", "s1", "p4", "d2", "s2",
+    "p5",
 )
 PLAY_E = (
-    "d3", "s2", "s3", "s4", "s5",
+    "d3", "s3", "s4", "s5",
 )
 PLAY_F = (
-    "m0", "00", "y0", "y1", "m1", "01", "y2", "x0", "m2", "02", "y3", "x1", "m3", "03", "y4",
-    "f0", "m4", "04", "y5", "x2", "m5", "05",
+    "y0", "y1", "m0", "00", "y2", "x0", "m1", "01", "y3", "x1", "m3", "03", "y4", "x2", "m4",
+    "04", "y5", "f0", "m5", "05", "d5", "m2", "02",
 )
 PLAY_G = (
-    "f1", "x3", "10", "f2", "11", "x4",
+    "x3", "f1", "10", "x4", "11", "x5",
 )
 PLAY_H = (
-    "f3", "12", "x5", "f4", "13", "f5",
+    "f3", "13", "f4", "14", "f5", "15", "f2", "12",
 )
 
 
@@ -58,10 +62,9 @@
     th_own, sh_own, codes, scales, weight, loss_in,
     kl_out, gh_out, gw_out,
     th, sh, table, wgt, wgt_t, tlog, slog, lsc, stat, stat_b, fin, in_a, in_b,
-    grad, gw_buf, mine, theirs, core_in,
+    grad, mine, theirs, core_in,
     y1s, y1r, x1s, x1r, x2s, x2r, y2s, y2r, zs, zr, zf,
-    sc_rows, loss_row, ld_sem, gw_sem, pc_s, pc_r, hop_s, hop_r,
-    ls_s, ls_r, a_s, a_r, b_s, b_r, cs, cr, r1s, r1r, r2s, r2r, z_ss, z_rs,
+    sc_rows, loss_row, ld_sem, pc_r, hop_r, sent, ls_r, a_r, b_r, cr, r1r, r2r, z_rs,
 ):
     v, d = lax.axis_index("vocab"), lax.axis_index("dp")
     core, y = lax.rem(d, 2), lax.div(d, 2)
@@ -76,9 +79,9 @@
     span = n_y * tok
     quarter = tok // 4
 
-    def rcopy(src, dst, send, recv, dev):
+    def rcopy(src, dst, recv, dev):
         return pltpu.make_async_remote_copy(
-            src_ref=src, dst_ref=dst, send_sem=send, recv_sem=recv,
+            src_ref=src, dst_ref=dst, send_sem=sent, recv_sem=recv,
             device_id=dev, device_id_type=MESH,
         )
 
@@ -140,7 +143,7 @@
         pl.semaphore_wait(barrier, len(peers_a) + len(peers_b))
 
     A, B, C, E = 2 * r + p, 2 * r + 1 - p, 2 * (1 - r) + p, 2 * (1 - r) + 1 - p
-    Y_A, Y_E, X_A, Z_A, X_C, Z_B, D_A, D_B, D_C, D_E = range(10)
+    Y_A, X_A, Z_A, FAR, D_A, D_REST = range(6)
     order = []
     for i in range(n_z1):
         order += [i, n_z1 + i]
@@ -151,7 +154,6 @@
         mate = 2 * y + 1 - c
         X, Z = (v_pair, d), (v_quad, d)
         sends = []
-        gw_copies = []
 
         def launch(cp):
             cp.start()
@@ -176,52 +178,44 @@
             ]
             for o in range(1, n_y):
                 to = 2 * lax.rem(y + o, n_y) + c
-                launch(rcopy(
-                    src, region(c, k, y, piece),
-                    hop_s.at[kind, o - 1, k], hop_r.at[kind, o - 1, k], (v, to),
-                ))
-
-        def hop(kind, k, o, g, piece, dev, half=None):
-            ref = region(g, k, came(o), piece, half)
-            return rcopy(ref, ref, hop_s.at[kind, o - 1, k], hop_r.at[kind, o - 1, k], dev)
+                launch(rcopy(src, region(c, k, y, piece), hop_r.at[kind, o - 1, k], (v, to)))
+
+        def hop(kind, k, o, piece, dev, half=None):
+            ref = region(c, k, came(o), piece, half)
+            return rcopy(ref, ref, hop_r.at[kind, o - 1, k], dev)
 
         def to_mate(kind, k, o, piece):
-            launch(hop(kind, k, o, c, piece, (v, mate)))
+            launch(hop(kind, k, o, piece, (v, mate)))
 
         def stage_y(k):
             for o in range(1, n_y):
-                hop(Y_A, k, o, c, A, X).wait_recv()
-                launch(hop(X_A, k, o, c, A, X))
-                launch(hop(Z_A, k, o, c, A, Z))
+                hop(Y_A, k, o, A, X).wait_recv()
+                launch(hop(X_A, k, o, A, X))
+                launch(hop(Z_A, k, o, A, Z))
                 to_mate(D_A, k, o, A)
 
         def stage_xz(k):
             for o in range(1, n_y):
-                hop(X_A, k, o, c, B, X).wait_recv()
+                hop(X_A, k, o, B, X).wait_recv()
                 if not by_y[k]:
-                    launch(hop(Z_B, k, o, c, B, Z, 1))
-                to_mate(D_B, k, o, B)
-                hop(Z_A, k, o, c, C, Z).wait_recv()
+                    launch(hop(FAR, k, o, B, Z, 1))
+                to_mate(D_REST, k, o, B)
+                hop(Z_A, k, o, C, Z).wait_recv()
                 if not by_y[k]:
-                    launch(hop(X_C, k, o, c, C, X, 0))
-                to_mate(D_C, k, o, C)
+                    launch(hop(FAR, k, o, C, X, 0))
+                to_mate(D_REST, k, o, C)
 
         def stage_far(k):
             for o in range(1, n_y):
-                if by_y[k]:
-                    hop(Y_E, k, o, c, E, X).wait_recv()
-                else:
-                    hop(X_C, k, o, c, E, X, 0).wait_recv()
-                    hop(Z_B, k, o, c, E, Z, 1).wait_recv()
-                to_mate(D_E, k, o, E)
-
-        def mate_wait(k, pairs):
+                hop(FAR, k, o, E, X).wait_recv()
+                to_mate(D_REST, k, o, E)
+
+        def mate_wait(kind, k):
+            scr, base, width = chunks[k][1], chunks[k][4], chunks[k][5]
+            size = quarter if kind == D_A else 3 * quarter
             for o in range(1, n_y):
-                for kind, piece in pairs:
-                    hop(kind, k, o, 1 - c, piece, X).wait_recv()
-
-        first_pair = [(D_A, A)]
-        rest_pairs = [(D_B, B), (D_C, C), (D_E, E)]
+                ref = scr.at[pl.ds(block(1 - c, came(o)), size), pl.ds(base, width)]
+                rcopy(ref, ref, hop_r.at[kind, o - 1, k], X).wait_recv()
 
         def prepare(k, half):
             own, scr, tab, acc, base, width = chunks[k]
@@ -283,10 +277,10 @@
             return t_top, t_sum, x_sum, s_top, s_sum
 
         def a_copy(g, i):
-            return rcopy(stat.at[g], in_a.at[g, i], a_s.at[g, i], a_r.at[g, i], peers_a[i])
+            return rcopy(stat.at[g], in_a.at[g, i], a_r.at[g], peers_a[i])
 
         def b_copy(g, i):
-            return rcopy(stat_b.at[g], in_b.at[g, i], b_s.at[g, i], b_r.at[g, i], peers_b[i])
+            return rcopy(stat_b.at[g], in_b.at[g, i], b_r.at[g], peers_b[i])
 
         def send_a(g):
             local_stat(g)
@@ -294,8 +288,7 @@
                 launch(a_copy(g, i))
 
         def send_b(g):
-            for i in range(len(peers_a)):
-                a_copy(g, i).wait_recv()
+            rcopy(in_a.at[g], in_a.at[g], a_r.at[g], X).wait_recv()
             stat_b[g] = jnp.concatenate(
                 list(merge([stat[g]] + [in_a[g, i] for i in range(len(peers_a))]))
                 + [jnp.zeros((3, span), jnp.float32)], axis=0
@@ -304,8 +297,7 @@
                 launch(b_copy(g, i))
 
         def finish(g):
-            for i in range(len(peers_b)):
-                b_copy(g, i).wait_recv()
+            rcopy(in_b.at[g], in_b.at[g], b_r.at[g], X).wait_recv()
             t_top, t_sum, x_sum, s_top, s_sum = merge(
                 [stat_b[g]] + [in_b[g, i] for i in range(len(peers_b))]
             )
@@ -350,27 +342,22 @@
                 launch(core_copy(z))
 
         def core_copy(z):
-            return rcopy(theirs.at[z], core_in.at[z], cs.at[z], cr.at[z], (v, mate))
+            return rcopy(theirs.at[z], core_in.at[z], cr.at[z], (v, mate))
 
         def y1_copy(z, o):
             to = 2 * lax.rem(y + o, n_y) + c
-            return rcopy(
-                y1s.at[z, o - 1], y1r.at[z, o - 1], r1s.at[z, o - 1], r1r.at[z, o - 1], (v, to)
-            )
+            return rcopy(y1s.at[z, o - 1], y1r.at[z, o - 1], r1r.at[z, o - 1], (v, to))
 
         def x1_copy(z):
-            return rcopy(x1s.at[z], x1r.at[z], r2s.at[z, 0], r2r.at[z, 0], (v_pair, d))
+            return rcopy(x1s.at[z], x1r.at[z], r2r.at[z, 0], (v_pair, d))
 
         def x2_copy(z):
-            return rcopy(
-                x2s.at[z - n_z1], x2r.at[z - n_z1], r1s.at[z, 0], r1r.at[z, 0], (v_pair, d)
-            )
+            return rcopy(x2s.at[z - n_z1], x2r.at[z - n_z1], r1r.at[z, 0], (v_pair, d))
 
         def y2_copy(z, o):
             to = 2 * lax.rem(y + o, n_y) + c
             return rcopy(
-                y2s.at[z - n_z1, o - 1], y2r.at[z - n_z1, o - 1],
-                r2s.at[z, o - 1], r2r.at[z, o - 1], (v, to),
+                y2s.at[z - n_z1, o - 1], y2r.at[z - n_z1, o - 1], r2r.at[z, o - 1], (v, to),
             )
 
         def after_core(z):
@@ -419,7 +406,7 @@
                 zf[z] = total(y)
 
         def z_copy(z):
-            return rcopy(zs.at[z], zr.at[q], z_ss.at[z], z_rs.at[q], (2 * z + p, d))
+            return rcopy(zs.at[z], zr.at[lax.rem(q + n_z - z, n_z) - 1], z_rs, (2 * z + p, d))
 
         def after_second(z):
             if z < n_z1:
@@ -439,59 +426,42 @@
 
         def weight_part(b):
             sl = pl.ds(b * 512, 512)
-            gw_buf[:, sl] = jnp.dot(
+            gw_out[:, sl] = jnp.dot(
                 grad[...], sh[:, sl], preferred_element_type=jnp.float32
             ).astype(jnp.bfloat16)
-            cp = pltpu.make_async_copy(gw_buf.at[:, sl], gw_out.at[:, sl], gw_sem.at[b])
-            cp.start()
-            gw_copies.append(cp)
 
         def last():
             total = zf[q]
-            for o in range(1, n_z):
-                src = lax.rem(q + o, n_z)
-                rcopy(
-                    zs.at[src], zr.at[src], z_ss.at[src], z_rs.at[src], (v_pair, d)
-                ).wait_recv()
-                total += zr[src].astype(jnp.float32)
+            rcopy(zr, zr, z_rs, X).wait_recv()
+            for o in range(n_z - 1):
+                total += zr[o].astype(jnp.float32)
             gh_out[...] = total.astype(jnp.bfloat16)
 
         def loss_wait():
-            for dd in range(1, n_dp):
-                other = lax.rem(d + n_dp - dd, n_dp)
-                slot = lax.rem(other, 2) * n_y + lax.div(other, 2)
-                rcopy(
-                    loss_row, lsc.at[slot], ls_s.at[dd - 1], ls_r.at[dd - 1], (v, mate)
-                ).wait_recv()
+            got = lsc.at[pl.ds(0, n_dp - 1)]
+            rcopy(got, got, ls_r, X).wait_recv()
 
         def mate_copies():
             for i, (own, scr) in enumerate(((th_own, th), (sh_own, sh))):
-                launch(rcopy(
-                    own, scr.at[pl.ds(block(c, y), tok)], pc_s.at[i], pc_r.at[i], (v, mate)
-                ))
+                launch(rcopy(own, scr.at[pl.ds(block(c, y), tok)], pc_r.at[i], (v, mate)))
 
         def mate_arrived():
             for i, (own, scr) in enumerate(((th_own, th), (sh_own, sh))):
-                rcopy(
-                    own, scr.at[pl.ds(block(1 - c, y), tok)], pc_s.at[i], pc_r.at[i], (v, mate)
-                ).wait_recv()
+                rcopy(own, scr.at[pl.ds(block(1 - c, y), tok)], pc_r.at[i], (v, mate)).wait_recv()
 
         def named(name, fn, *args):
             with jax.named_scope(name + "_".join(str(x) for x in args if isinstance(x, int))):
                 fn(*args)
 
         for dd in range(1, n_dp):
-            launch(rcopy(
-                loss_row, lsc.at[c * n_y + y], ls_s.at[dd - 1], ls_r.at[dd - 1],
-                (v, lax.rem(d + dd, n_dp)),
-            ))
+            launch(rcopy(loss_row, lsc.at[c * n_y + y], ls_r, (v, lax.rem(d + dd, n_dp))))
         far = [k for k in range(n_ch) if by_y[k]]
 
         def send_y(k):
             y_send(k, Y_A)
             if k == n_ch - 1:
                 for kk in far:
-                    y_send(kk, Y_E)
+                    y_send(kk, FAR)
 
         ops = {
             "p": lambda k: prepare(k, 0),
@@ -500,8 +470,8 @@
             "y": stage_y,
             "x": stage_xz,
             "f": stage_far,
-            "d": lambda k: mate_wait(k, first_pair),
-            "m": lambda k: mate_wait(k, rest_pairs),
+            "d": lambda k: mate_wait(D_A, k),
+            "m": lambda k: mate_wait(D_REST, k),
             "0": lambda k: product(0, k),
             "1": lambda k: product(1, k),
         }
@@ -526,7 +496,7 @@
             named("mate_arrived", mate_arrived)
             play(PLAY_C, "")
             named("send_b", send_b, 0)
-            play((), "dm1")
+            play(PLAY_I, "dm1")
             named("send_a", send_a, 1)
             loss_wait()
             named("finish", finish, 0)
@@ -581,10 +551,7 @@
         for cp in sends:
             cp.wait_send()
         for o in range(1, n_z):
-            dst = lax.rem(q + o, n_z)
-            rcopy(zs.at[dst], zr.at[q], z_ss.at[dst], z_rs.at[q], (2 * dst + p, d)).wait_send()
-        for cp in gw_copies:
-            cp.wait()
+            z_copy(lax.rem(q + o, n_z)).wait_send()
 
     for which in range(2):
         pl.when(core == which)(functools.partial(run, which))
@@ -594,30 +561,26 @@
     parts = 4
     step = gw.shape[0] // parts
 
-    def move(kl_in, gh_in, gw_in, kl_to, gh_to, gw_to, kl_v, gh_v, gw_v, sem_in, sem_out):
-        plan = [(kl_in, kl_v, kl_to), (gh_in, gh_v, gh_to)]
+    def move(kl_in, gh_in, gw_in, kl_to, gh_to, gw_to, sem):
+        plan = [(gh_in, gh_to), (kl_in, kl_to)]
         for i in range(parts):
             sl = pl.ds(i * step, step)
-            plan.append((gw_in.at[sl], gw_v.at[sl], gw_to.at[sl]))
-        reads = [pltpu.make_async_copy(a, b, sem_in.at[i]) for i, (a, b, _) in enumerate(plan)]
-        writes = [pltpu.make_async_copy(b, e, sem_out.at[i]) for i, (_, b, e) in enumerate(plan)]
-        for cp in reads:
+            plan.append((gw_in.at[sl], gw_to.at[sl]))
+        writes = [pltpu.make_async_copy(a, b, sem.at[i]) for i, (a, b) in enumerate(plan)]
+        for cp in writes:
             cp.start()
-        for cp, out in zip(reads, writes):
+        for cp in writes:
             cp.wait()
-            out.start()
-        for out in writes:
-            out.wait()
 
     spec = pl.BlockSpec(memory_space=pl.ANY)
     arrays = (kl, gh, gw)
     return pl.pallas_call(
         move,
         out_shape=tuple(jax.ShapeDtypeStruct(a.shape, a.dtype) for a in arrays),
-        in_specs=[spec] * 3,
+        in_specs=[pl.BlockSpec(memory_space=pltpu.VMEM)] * 3,
         out_specs=(spec,) * 3,
-        scratch_shapes=[pltpu.VMEM(a.shape, a.dtype) for a in arrays]
-        + [pltpu.SemaphoreType.DMA((parts + 2,))] * 2,
+        scratch_shapes=[pltpu.SemaphoreType.DMA((parts + 2,))],
+        compiler_params=pltpu.CompilerParams(vmem_limit_bytes=4 * 1024 * 1024),
         name="hand_over",
     )(*arrays)
 
@@ -644,33 +607,31 @@
         kl, gh, gw = pl.pallas_call(
             functools.partial(kernel, n_vocab, n_dp),
             out_shape=(
-                jax.ShapeDtypeStruct((1, tok), f32),
-                jax.ShapeDtypeStruct((rv, tok), bf),
-                jax.ShapeDtypeStruct((rows, ds_), bf),
+                pltpu.VMEM((1, tok), f32),
+                pltpu.VMEM((rv, tok), bf),
+                pltpu.VMEM((rows, ds_), bf),
             ),
             in_specs=[any_spec, any_spec, any_spec, vm_spec, any_spec, vm_spec],
-            out_specs=(vm_spec, vm_spec, any_spec),
+            out_specs=(vm_spec, vm_spec, vm_spec),
             scratch_shapes=[
                 V((n_tok, dt), bf), V((n_tok, ds_), bf), V((rows, dt), bf), V((rows, ds_), bf),
                 V((ds_, rows), bf), V((rows, n_tok), f32), V((rows, n_tok), f32),
                 V((n_dp, 8, tok), f32), V((2, 8, span), f32), V((2, 8, span), f32),
                 V((2, 8, span), f32), V((2, n_a, 8, span), f32), V((2, n_b, 8, span), f32),
-                V((rows, n_tok), bf), V((rows, ds_), bf),
+                V((rows, n_tok), bf),
                 V((n_z, 2, n_y, rv, tok), f32), V((n_z, 2, n_y, rv, tok), bf),
                 V((n_z, 2, n_y, rv, tok), bf),
                 V((n_z1, n_off, 2, rv, tok), bf), V((n_z1, n_off, 2, rv, tok), bf),
                 V((n_z1, rv, tok), bf), V((n_z1, rv, tok), bf),
                 V((n_z2, n_y, rv, tok), bf), V((n_z2, n_y, rv, tok), bf),
                 V((n_z2, n_off, rv, tok), bf), V((n_z2, n_off, rv, tok), bf),
-                V((n_z, rv, tok), bf), V((n_z, rv, tok), bf), V((n_z, rv, tok), f32),
+                V((n_z, rv, tok), bf), V((n_z - 1, rv, tok), bf), V((n_z, rv, tok), f32),
                 V((rows, -(-scales.shape[1] // 8) * 8), f32), V((8, tok), f32),
-                D((n_ch + 2,)), D((ds_ // 512,)), D((2,)), D((2,)),
-                D((10, n_off, n_ch)), D((10, n_off, n_ch)),
-                D((n_dp - 1,)), D((n_dp - 1,)), *[D((2, n_a))] * 2, *[D((2, n_b))] * 2,
-                D((n_z,)), D((n_z,)), *[D((n_z, n_off))] * 4, D((n_z,)), D((n_z,)),
+                D((n_ch + 2,)), D((2,)), D((6, n_off, n_ch)), D, D, D((2,)), D((2,)),
+                D((n_z,)), D((n_z, n_off)), D((n_z, n_off)), D,
             ],
             compiler_params=pltpu.CompilerParams(
-                collective_id=0, has_side_effects=True, vmem_limit_bytes=60 * 1024 * 1024
+                collective_id=0, has_side_effects=True, vmem_limit_bytes=56 * 1024 * 1024
             ),
             name="distill",
         )(th_own, sh_own, codes, scales.T, weight, loss_scale)

time: 60.8 us -> 56.3 us (0.926)
  Pallas kernels: 59.8 us -> 55.4 us
    pallas_call x1, Pallas kernels: 57.1 us -> 53.8 us  [local(): pl.pallas_call(functools.partial(kernel, n_vocab, n_dp), out_shape=(pltpu...]
    pallas_call x1, Pallas kernels: 2.73 us -> 1.57 us  [hand_over(): pl.pallas_call(move, out_shape=tuple((jax.ShapeDtypeStruct(a.shape, a.dty...]
where the time goes in v2:
time: 56.3 us; the launch traced here: 56.2 us
  Pallas kernels  55.4 us (98%)
  between operations  0.8 us (1%)
    pallas_call x1, Pallas kernels, local(): pl.pallas_call(functools.partial(kernel, n_vocab, n_dp), out_shape=(pltpu...  53.8 us
    pallas_call x1, Pallas kernels, hand_over(): pl.pallas_call(move, out_shape=tuple((jax.ShapeDtypeStruct(a.shape, a.dty...  1.57 us

profile of v2, /device:TPU:1, one launch (start us, length us, event | category | flops | bytes accessed | tf_op | source)
XLA Modules:
  0.0 56.2 jit_solution(7782250470965213627)
XLA Ops:
  0.6 53.8 %distill.1 = (f32[1,128]{1,0:T(1,128)S(1)}, bf16[320,128]{1,0:T(8,128)(2,1)S(1)}, bf16[512,2560]{1,0:T(8,128)(2,1)S(1)}) custom-call(bf16[128,5376]{1,0:T(8,128)(2,1)} %th_own.1, bf16[128,2560]{1,0:T(8,128)(2,1)} %sh_own.1, bf16[512,5376]{1,0:T(8,128)(2,1)} %codes.1, f32[42,512]{1,0:T(8,128)} %bitcast.3, bf16[512,2560]{1,0:T(8,128)(2,1)} %weight.1, ...), custom_call_target="tpu_custom_call" | custom-call | tf_op jit(solution)/shard_map/distill/pallas_call | solution.py:607
  54.5 1.6 %hand_over.1 = (f32[1,128]{1,0:T(1,128)}, bf16[320,128]{1,0:T(8,128)(2,1)}, bf16[512,2560]{1,0:T(8,128)(2,1)}) custom-call(f32[1,128]{1,0:T(1,128)S(1)} %get-tuple-element.9.kl_in, bf16[320,128]{1,0:T(8,128)(2,1)S(1)} %get-tuple-element.10.gh_in, bf16[512,2560]{1,0:T(8,128)(2,1)S(1)} %get-tuple-element.11.gw_in), custom_call_target="tpu_custom_call" | custom-call | tf_op jit(solution)/shard_map/hand_over/pallas_call | solution.py:577

commit v3 on v2

--- a/solution.py
+++ b/solution.py
@@ -16,10 +16,10 @@
 )
 PLAY_B = (
     "y0", "q2", "y1", "p3", "y2", "q3", "y3", "x0", "y4", "x1", "y5", "p4", "p5", "x2", "f0",
-    "00", "x3", "f1", "01", "x4", "f3", "03", "x5", "f4", "04", "f5", "05", "f2", "02",
+    "00", "x3", "f3", "03", "f1", "01", "x4", "f4", "04", "x5", "f5", "05", "f2", "02",
 )
 PLAY_C = (
-    "d0", "m0", "10", "d1", "m1", "11",
+    "d0", "m0", "10", "d1", "m1", "11", "d2", "m2", "12",
 )
 PLAY_I = (
     "d3", "m3", "13", "d4", "m4", "14", "d5", "m5", "15",
@@ -29,17 +29,17 @@
     "p5",
 )
 PLAY_E = (
-    "d3", "s3", "s4", "s5",
+    "d3", "s3", "s4", "s5", "y0", "d4", "y1", "d5",
 )
 PLAY_F = (
-    "y0", "y1", "m0", "00", "y2", "x0", "m1", "01", "y3", "x1", "m3", "03", "y4", "x2", "m4",
-    "04", "y5", "f0", "m5", "05", "d5", "m2", "02",
+    "x0", "y2", "m0", "00", "m3", "03", "m1", "01", "y3", "x1", "y4", "m4", "04", "x2", "f0",
+    "y5", "m5", "05", "m2", "02",
 )
 PLAY_G = (
-    "x3", "f1", "10", "x4", "11", "x5",
+    "x3", "10", "f1", "x4", "11", "f2", "12", "x5", "f3",
 )
 PLAY_H = (
-    "f3", "13", "f4", "14", "f5", "15", "f2", "12",
+    "f4", "13", "f5", "14", "15",
 )
 
 
@@ -240,11 +240,14 @@
             own, scr, tab, acc, base, width = chunks[k]
             for b in range(g * span, (g + 1) * span, 2 * tok):
                 two = pl.ds(b, 2 * tok)
-                part = dot_t(tab[:, pl.ds(base, width)], scr[two, pl.ds(base, width)])
-                if firsts[k]:
-                    acc[:, two] = part
-                else:
-                    acc[:, two] += part
+                half = tab.shape[0] // 2
+                for h in range(2):
+                    top = pl.ds(h * half, half)
+                    part = dot_t(tab[top, pl.ds(base, width)], scr[two, pl.ds(base, width)])
+                    if firsts[k]:
+                        acc[top, two] = part
+                    else:
+                        acc[top, two] += part
 
         def local_stat(g):
             @pl.loop(0, n_y)
@@ -506,10 +509,12 @@
                     named("after_core", after_core, order[i - 1])
             named("after_core", after_core, order[-1])
             named("send_b", send_b, 1)
+            for z in order[:2]:
+                named("after_first", after_first, z)
             named("finish", finish, 1)
             for z in order:
                 named("hidden", hidden, 1, z)
-            for z in order:
+            for z in order[2:]:
                 named("after_first", after_first, z)
             for b in range(n_gw):
                 named("weight", weight_part, b)

time: 56.3 us -> 53.3 us (0.947)
  Pallas kernels: 55.4 us -> 52.4 us
    pallas_call x1, Pallas kernels: 53.8 us -> 50.8 us  [local(): pl.pallas_call(functools.partial(kernel, n_vocab, n_dp), out_shape=(pltpu...]
where the time goes in v3:
time: 53.3 us; the launch traced here: 53.2 us
  Pallas kernels  52.4 us (98%)
  between operations  0.8 us (2%)
    pallas_call x1, Pallas kernels, local(): pl.pallas_call(functools.partial(kernel, n_vocab, n_dp), out_shape=(pltpu...  50.8 us
    pallas_call x1, Pallas kernels, hand_over(): pl.pallas_call(move, out_shape=tuple((jax.ShapeDtypeStruct(a.shape, a.dty...  1.57 us

profile of v3, /device:TPU:1, one launch (start us, length us, event | category | flops | bytes accessed | tf_op | source)
XLA Modules:
  0.0 53.2 jit_solution(14407181548249835783)
XLA Ops:
  0.6 50.8 %distill.1 = (f32[1,128]{1,0:T(1,128)S(1)}, bf16[320,128]{1,0:T(8,128)(2,1)S(1)}, bf16[512,2560]{1,0:T(8,128)(2,1)S(1)}) custom-call(bf16[128,5376]{1,0:T(8,128)(2,1)} %th_own.1, bf16[128,2560]{1,0:T(8,128)(2,1)} %sh_own.1, bf16[512,5376]{1,0:T(8,128)(2,1)} %codes.1, f32[42,512]{1,0:T(8,128)} %bitcast.3, bf16[512,2560]{1,0:T(8,128)(2,1)} %weight.1, ...), custom_call_target="tpu_custom_call" | custom-call | tf_op jit(solution)/shard_map/distill/pallas_call | solution.py:612
  51.4 1.6 %hand_over.1 = (f32[1,128]{1,0:T(1,128)}, bf16[320,128]{1,0:T(8,128)(2,1)}, bf16[512,2560]{1,0:T(8,128)(2,1)}) custom-call(f32[1,128]{1,0:T(1,128)S(1)} %get-tuple-element.9.kl_in, bf16[320,128]{1,0:T(8,128)(2,1)S(1)} %get-tuple-element.10.gh_in, bf16[512,2560]{1,0:T(8,128)(2,1)S(1)} %get-tuple-element.11.gw_in), custom_call_target="tpu_custom_call" | custom-call | tf_op jit(solution)/shard_map/hand_over/pallas_call | solution.py:582

commit v4 on v3

--- a/solution.py
+++ b/solution.py
@@ -62,9 +62,9 @@
     th_own, sh_own, codes, scales, weight, loss_in,
     kl_out, gh_out, gw_out,
     th, sh, table, wgt, wgt_t, tlog, slog, lsc, stat, stat_b, fin, in_a, in_b,
-    grad, mine, theirs, core_in,
+    grad, grad_m, wgt_m, tl_m, sl_m, mine,
     y1s, y1r, x1s, x1r, x2s, x2r, y2s, y2r, zs, zr, zf,
-    sc_rows, loss_row, ld_sem, pc_r, hop_r, sent, ls_r, a_r, b_r, cr, r1r, r2r, z_rs,
+    sc_rows, loss_row, ld_sem, pc_r, hop_r, sent, ls_r, a_r, b_r, w_r, e_r, r1r, r2r, z_rs,
 ):
     v, d = lax.axis_index("vocab"), lax.axis_index("dp")
     core, y = lax.rem(d, 2), lax.div(d, 2)
@@ -146,13 +146,14 @@
     Y_A, X_A, Z_A, FAR, D_A, D_REST = range(6)
     order = []
     for i in range(n_z1):
-        order += [i, n_z1 + i]
+        order += [i, n_z - 1 - i]
     order += [i for i in range(n_z) if i not in order]
     n_gw = sh.shape[1] // 512
 
     def run(c):
         mate = 2 * y + 1 - c
         X, Z = (v_pair, d), (v_quad, d)
+        mate_slot = 0 if c == 1 else n_dp - 2
         sends = []
 
         def launch(cp):
@@ -285,10 +286,23 @@
         def b_copy(g, i):
             return rcopy(stat_b.at[g], in_b.at[g, i], b_r.at[g], peers_b[i])
 
+        def exp_copies(g):
+            sl = pl.ds(g * span, span)
+            return [
+                rcopy(tlog.at[:, sl], tl_m, e_r.at[0], (v, mate)),
+                rcopy(slog.at[:, sl], sl_m, e_r.at[1], (v, mate)),
+            ]
+
+        def weight_copy():
+            return rcopy(wgt_t, wgt_m, w_r, (v, mate))
+
         def send_a(g):
             local_stat(g)
             for i in reversed(range(len(peers_a))):
                 launch(a_copy(g, i))
+            if g != c:
+                for cp in exp_copies(g):
+                    launch(cp)
 
         def send_b(g):
             rcopy(in_a.at[g], in_a.at[g], a_r.at[g], X).wait_recv()
@@ -311,12 +325,16 @@
                     x_sum / t_sum - t_lse + s_lse,
                     jnp.exp(stat[g, 0:1] - t_lse),
                     jnp.exp(stat[g, 3:4] - s_lse),
-                    jnp.zeros((5, span), jnp.float32),
+                    jnp.exp(in_a[g, mate_slot, 0:1] - t_lse),
+                    jnp.exp(in_a[g, mate_slot, 3:4] - s_lse),
+                    jnp.zeros((3, span), jnp.float32),
                 ],
                 axis=0,
             )
             if g == c:
                 kl_out[...] = fin[g, 0:1, pl.ds(pl.multiple_of(y * tok, tok), tok)]
+                for cp in exp_copies(g):
+                    cp.wait_recv()
 
             @pl.loop(0, n_y)
             def _(j):
@@ -326,26 +344,25 @@
                 grad[:, sl] = (
                     lsc[g * n_y + j][0:1] * (slog[:, sl] * f[2:3] - tlog[:, sl] * f[1:2])
                 ).astype(jnp.bfloat16)
-
-        def hidden(g, z):
+                if g == c:
+                    at = pl.ds(off, tok)
+                    grad_m[:, at] = (
+                        lsc[g * n_y + j][0:1] * (sl_m[:, at] * f[4:5] - tl_m[:, at] * f[3:4])
+                    ).astype(jnp.bfloat16)
+
+        def hidden(z):
             for pp in range(2):
-                feat = wgt_t[pl.ds((2 * z + pp) * rv, rv), :]
+                at = pl.ds((2 * z + pp) * rv, rv)
                 for yy in range(0, n_y, 2):
                     part = jnp.dot(
-                        feat, grad[:, pl.ds(g * span + yy * tok, 2 * tok)],
+                        wgt_t[at, :], grad[:, pl.ds(c * span + yy * tok, 2 * tok)],
+                        preferred_element_type=jnp.float32,
+                    ) + jnp.dot(
+                        wgt_m[at, :], grad_m[:, pl.ds(yy * tok, 2 * tok)],
                         preferred_element_type=jnp.float32,
                     )
                     for h in range(2):
-                        one = part[:, h * tok : (h + 1) * tok]
-                        if g == c:
-                            mine[z, pp, yy + h] = one
-                        else:
-                            theirs[z, pp, yy + h] = one.astype(jnp.bfloat16)
-            if g != c:
-                launch(core_copy(z))
-
-        def core_copy(z):
-            return rcopy(theirs.at[z], core_in.at[z], cr.at[z], (v, mate))
+                        mine[z, pp, yy + h] = part[:, h * tok : (h + 1) * tok]
 
         def y1_copy(z, o):
             to = 2 * lax.rem(y + o, n_y) + c
@@ -363,21 +380,16 @@
                 y2s.at[z - n_z1, o - 1], y2r.at[z - n_z1, o - 1], r2r.at[z, o - 1], (v, to),
             )
 
-        def after_core(z):
-            core_copy(z).wait_recv()
+        def first_sends(z):
             if z < n_z1:
                 for o in range(1, n_y):
                     to = lax.rem(y + o, n_y)
                     for pp in range(2):
-                        y1s[z, o - 1, pp] = (
-                            mine[z, pp, to] + core_in[z, pp, to].astype(jnp.float32)
-                        ).astype(jnp.bfloat16)
+                        y1s[z, o - 1, pp] = mine[z, pp, to].astype(jnp.bfloat16)
                     launch(y1_copy(z, o))
             else:
                 for yy in range(n_y):
-                    x2s[z - n_z1, yy] = (
-                        mine[z, 1 - p, yy] + core_in[z, 1 - p, yy].astype(jnp.float32)
-                    ).astype(jnp.bfloat16)
+                    x2s[z - n_z1, yy] = mine[z, 1 - p, yy].astype(jnp.bfloat16)
                 launch(x2_copy(z))
 
         def after_first(z):
@@ -386,7 +398,7 @@
                     y1_copy(z, o).wait_recv()
 
                 def total(which):
-                    out = mine[z, which, y] + core_in[z, which, y].astype(jnp.float32)
+                    out = mine[z, which, y]
                     for o in range(1, n_y):
                         out += y1r[z, o - 1, which].astype(jnp.float32)
                     return out
@@ -398,10 +410,7 @@
                 x2_copy(z).wait_recv()
 
                 def total(yy):
-                    return (
-                        mine[z, p, yy] + core_in[z, p, yy].astype(jnp.float32)
-                        + x2r[z - n_z1, yy].astype(jnp.float32)
-                    )
+                    return mine[z, p, yy] + x2r[z - n_z1, yy].astype(jnp.float32)
 
                 for o in range(1, n_y):
                     y2s[z - n_z1, o - 1] = total(lax.rem(y + o, n_y)).astype(jnp.bfloat16)
@@ -496,6 +505,7 @@
                 cp.wait()
             play(PLAY_B, "spqyxf0")
             named("send_a", send_a, 0)
+            launch(weight_copy())
             named("mate_arrived", mate_arrived)
             play(PLAY_C, "")
             named("send_b", send_b, 0)
@@ -503,19 +513,14 @@
             named("send_a", send_a, 1)
             loss_wait()
             named("finish", finish, 0)
-            for i, z in enumerate(order):
-                named("hidden", hidden, 0, z)
-                if i >= 1:
-                    named("after_core", after_core, order[i - 1])
-            named("after_core", after_core, order[-1])
+            weight_copy().wait_recv()
+            for z in order:
+                named("hidden", hidden, z)
+                named("first_sends", first_sends, z)
             named("send_b", send_b, 1)
-            for z in order[:2]:
+            for z in order:
                 named("after_first", after_first, z)
             named("finish", finish, 1)
-            for z in order:
-                named("hidden", hidden, 1, z)
-            for z in order[2:]:
-                named("after_first", after_first, z)
             for b in range(n_gw):
                 named("weight", weight_part, b)
             for z in order:
@@ -523,6 +528,10 @@
             named("last", last)
         else:
             mate_copies()
+            for k in range(n_ch):
+                if chunks[k][2] is wgt:
+                    play((f"p{k}",), "")
+            launch(weight_copy())
             play(PLAY_D, "pq")
             for cp in own_loads:
                 cp.wait()
@@ -536,15 +545,12 @@
             named("send_a", send_a, 1)
             loss_wait()
             named("finish", finish, 0)
+            named("send_b", send_b, 1)
+            weight_copy().wait_recv()
+            named("finish", finish, 1)
             for z in order:
-                named("hidden", hidden, 0, z)
-            named("send_b", send_b, 1)
-            named("finish", finish, 1)
-            for i, z in enumerate(order):
-                named("hidden", hidden, 1, z)
-                if i >= 1:
-                    named("after_core", after_core, order[i - 1])
-            named("after_core", after_core, order[-1])
+                named("hidden", hidden, z)
+                named("first_sends", first_sends, z)
             for b in range(n_gw):
                 named("weight", weight_part, b)
             for z in order:
@@ -624,8 +630,8 @@
                 V((n_dp, 8, tok), f32), V((2, 8, span), f32), V((2, 8, span), f32),
                 V((2, 8, span), f32), V((2, n_a, 8, span), f32), V((2, n_b, 8, span), f32),
                 V((rows, n_tok), bf),
-                V((n_z, 2, n_y, rv, tok), f32), V((n_z, 2, n_y, rv, tok), bf),
-                V((n_z, 2, n_y, rv, tok), bf),
+                V((rows, span), bf), V((ds_, rows), bf), V((rows, span), f32),
+                V((rows, span), f32), V((n_z, 2, n_y, rv, tok), f32),
                 V((n_z1, n_off, 2, rv, tok), bf), V((n_z1, n_off, 2, rv, tok), bf),
                 V((n_z1, rv, tok), bf), V((n_z1, rv, tok), bf),
                 V((n_z2, n_y, rv, tok), bf), V((n_z2, n_y, rv, tok), bf),
@@ -633,7 +639,7 @@
                 V((n_z, rv, tok), bf), V((n_z - 1, rv, tok), bf), V((n_z, rv, tok), f32),
                 V((rows, -(-scales.shape[1] // 8) * 8), f32), V((8, tok), f32),
                 D((n_ch + 2,)), D((2,)), D((6, n_off, n_ch)), D, D, D((2,)), D((2,)),
-                D((n_z,)), D((n_z, n_off)), D((n_z, n_off)), D,
+                D, D((2,)), D((n_z, n_off)), D((n_z, n_off)), D,
             ],
             compiler_params=pltpu.CompilerParams(
                 collective_id=0, has_side_effects=True, vmem_limit_bytes=56 * 1024 * 1024

time: 53.3 us -> 52.1 us (0.977)
  Pallas kernels: 52.4 us -> 51.2 us
    pallas_call x1, Pallas kernels: 50.8 us -> 49.6 us  [local(): pl.pallas_call(functools.partial(kernel, n_vocab, n_dp), out_shape=(pltpu...]
where the time goes in v4:
time: 52.1 us; the launch traced here: 52 us
  Pallas kernels  51.2 us (98%)
  between operations  0.8 us (2%)
    pallas_call x1, Pallas kernels, local(): pl.pallas_call(functools.partial(kernel, n_vocab, n_dp), out_shape=(pltpu...  49.6 us
    pallas_call x1, Pallas kernels, hand_over(): pl.pallas_call(move, out_shape=tuple((jax.ShapeDtypeStruct(a.shape, a.dty...  1.57 us

profile of v4, /device:TPU:1, one launch (start us, length us, event | category | flops | bytes accessed | tf_op | source)
XLA Modules:
  0.0 52.0 jit_solution(116271458510142481)
XLA Ops:
  0.6 49.6 %distill.1 = (f32[1,128]{1,0:T(1,128)S(1)}, bf16[320,128]{1,0:T(8,128)(2,1)S(1)}, bf16[512,2560]{1,0:T(8,128)(2,1)S(1)}) custom-call(bf16[128,5376]{1,0:T(8,128)(2,1)} %th_own.1, bf16[128,2560]{1,0:T(8,128)(2,1)} %sh_own.1, bf16[512,5376]{1,0:T(8,128)(2,1)} %codes.1, f32[42,512]{1,0:T(8,128)} %bitcast.3, bf16[512,2560]{1,0:T(8,128)(2,1)} %weight.1, ...), custom_call_target="tpu_custom_call" | custom-call | tf_op jit(solution)/shard_map/distill/pallas_call | solution.py:618
  50.2 1.6 %hand_over.1 = (f32[1,128]{1,0:T(1,128)}, bf16[320,128]{1,0:T(8,128)(2,1)}, bf16[512,2560]{1,0:T(8,128)(2,1)}) custom-call(f32[1,128]{1,0:T(1,128)S(1)} %get-tuple-element.9.kl_in, bf16[320,128]{1,0:T(8,128)(2,1)S(1)} %get-tuple-element.10.gh_in, bf16[512,2560]{1,0:T(8,128)(2,1)S(1)} %get-tuple-element.11.gw_in), custom_call_target="tpu_custom_call" | custom-call | tf_op jit(solution)/shard_map/hand_over/pallas_call | solution.py:588
